TPU v7x, 32 devices: a whole 2x2x4 slice. The times are simulated.
32 devices in a mesh: rep: 2 (over x), shard: 4 (over y, core), ctx: 4 (over z).
Axes of the slice: x: 2, y: 2, z: 4, core: 2. Of those that a mesh axis runs over, the one named last changes fastest.
Arguments:
- tokens: bfloat16 [16, 256, 1024], P(('rep', 'shard'), 'ctx'), may hold values from -6 to 6
- positions: int32 [16, 256], P(('rep', 'shard')), may hold values from 0 to 255, as said below
- segments: int32 [16, 256], P(('rep', 'shard')), may hold values from 0 to 2, as said below
- cotangent: bfloat16 [16, 256, 1024], P(('rep', 'shard'), 'ctx'), may hold values from -6 to 6
- w_query: bfloat16 [1024, 2048], P(None, ('shard', 'ctx')), may hold values from -0.1875 to 0.1875
- key_weight: bfloat16 [1024, 1024], P(None, ('shard', 'ctx')), may hold values from -0.1875 to 0.1875
- value_weight: bfloat16 [1024, 1024], P(None, ('shard', 'ctx')), may hold values from -0.1875 to 0.1875
- output_weight: bfloat16 [2048, 1024], P(('shard', 'ctx')), may hold values from -0.625 to 0.625
- w_gate: bfloat16 [1024, 3072], P(None, ('shard', 'ctx')), may hold values from -0.1875 to 0.1875
- w_up: bfloat16 [1024, 3072], P(None, ('shard', 'ctx')), may hold values from -0.1875 to 0.1875
- w_down: bfloat16 [3072, 1024], P(('shard', 'ctx')), may hold values from -0.109375 to 0.109375
- norm_gains: bfloat16 [2304], P(('shard', 'ctx')), may hold values from 0.5 to 1.5
Outputs:
- block_out: bfloat16 [16, 256, 1024], P(('rep', 'shard'), 'ctx')
- grad_input: float32 [16, 256, 1024], P(('rep', 'shard'), 'ctx')
- grad_query: float32 [1024, 2048], P(None, ('shard', 'ctx'))
- grad_key: float32 [1024, 1024], P(None, ('shard', 'ctx'))
- grad_value: float32 [1024, 1024], P(None, ('shard', 'ctx'))
- grad_output: float32 [2048, 1024], P(('shard', 'ctx'))
- grad_gate: float32 [1024, 3072], P(None, ('shard', 'ctx'))
- grad_up: float32 [1024, 3072], P(None, ('shard', 'ctx'))
- grad_down: float32 [3072, 1024], P(('shard', 'ctx'))
- grad_gains: float32 [2304], P(('shard', 'ctx'))
Inputs may be any that keep to these rules, and one draw needn't show every extreme that they name: In each sequence the stored positions are a permutation of all its positions made of runs of 32 consecutive positions; the two runs held by one index of ctx are the k-th from the start and the k-th from the end of the sequence, with k drawn per sequence. `segments`: ordered by position, a sequence's document numbers never fall, start at 0 and use every number up to 2.
All inputs are finite; a program needn't handle non-finite values.
Results may differ from a plain program's by a relative error of at most 0.02.
Values may be sent and summed in bfloat16 or wider, within the bound.
A program may use at most 192 MiB of HBM per device.

v0:
```python
import functools
import math

import jax
import jax.numpy as jnp
from jax import lax
from jax.experimental import pallas as pl
from jax.experimental.pallas import tpu as pltpu
from jax.sharding import PartitionSpec as P

QUERY_HEADS = 16
KEY_VALUE_HEADS = 8
HEAD_DIM = 128

MESH = pl.DeviceIdType.MESH

EPSILON = 1e-06
ROPE_BASE = 1000000.0


def rms_scale(values_in):
    return lax.rsqrt(jnp.mean(values_in * values_in, axis=-1, keepdims=True) + EPSILON)


def norm_backward(grad_in, values_in, scale_in, gain_in):
    grad_norm = grad_in * gain_in
    unit = values_in * scale_in
    return scale_in * (grad_norm - unit * jnp.mean(grad_norm * unit, axis=-1, keepdims=True))


def rope_tables(position_ids):
    half_dim = HEAD_DIM // 2
    inverse = 1.0 / ROPE_BASE ** (jnp.arange(half_dim, dtype=jnp.float32) * (2.0 / HEAD_DIM))
    angle = position_ids.astype(jnp.float32)[..., None] * inverse
    return (jnp.cos(angle)[:, :, None, :], jnp.sin(angle)[:, :, None, :])


def rotate(values_in, cosine, sine):
    half_dim = values_in.shape[-1] // 2
    first = values_in[..., :half_dim]
    second = values_in[..., half_dim:]
    return jnp.concatenate(
        [first * cosine - second * sine, second * cosine + first * sine], axis=-1
    )


def rotate_back(grad_in, cosine, sine):
    half_dim = grad_in.shape[-1] // 2
    first = grad_in[..., :half_dim]
    second = grad_in[..., half_dim:]
    return jnp.concatenate(
        [first * cosine + second * sine, second * cosine - first * sine], axis=-1
    )


def float_product(left, right):
    return jnp.dot(left, right, preferred_element_type=jnp.float32)


def against_rows(left, right):
    return lax.dot_general(
        left, right, (((1,), (1,)), ((), ())), preferred_element_type=jnp.float32
    )


def over_tokens(left, right):
    return lax.dot_general(
        left, right, (((0,), (0,)), ((), ())), preferred_element_type=jnp.float32
    )


def body(
    tokens,
    positions,
    segments,
    cotangent,
    w_query,
    key_weight,
    value_weight,
    output_weight,
    w_gate,
    w_up,
    w_down,
    norm_gains,
):
    sequence_count, local_length, model_width = tokens.shape
    total_rows = sequence_count * local_length
    group_width = QUERY_HEADS // KEY_VALUE_HEADS
    score_scale = 1.0 / math.sqrt(HEAD_DIM)
    local_start = lax.axis_index("ctx") * local_length
    local_pos = lax.dynamic_slice_in_dim(positions, local_start, local_length, 1)
    local_seg = lax.dynamic_slice_in_dim(segments, local_start, local_length, 1)
    wq_full, full_key_weight, full_value_weight, wo_full, gains_full = (
        lax.all_gather(w_query, ("shard", "ctx"), axis=1, tiled=True),
        lax.all_gather(key_weight, ("shard", "ctx"), axis=1, tiled=True),
        lax.all_gather(value_weight, ("shard", "ctx"), axis=1, tiled=True),
        lax.all_gather(output_weight, ("shard", "ctx"), axis=0, tiled=True),
        lax.all_gather(norm_gains, ("shard", "ctx"), axis=0, tiled=True),
    )
    gain_all = gains_full.astype(jnp.float32)
    g_attn = gain_all[:model_width]
    g_query = gain_all[model_width : model_width + HEAD_DIM]
    key_gain = gain_all[model_width + HEAD_DIM : model_width + 2 * HEAD_DIM]
    g_mlp = gain_all[model_width + 2 * HEAD_DIM :]
    x_rows = tokens.reshape(total_rows, model_width).astype(jnp.float32)
    scale_in = rms_scale(x_rows)
    normed_input = (x_rows * scale_in * g_attn).astype(jnp.bfloat16)
    query = float_product(normed_input, wq_full).reshape(
        sequence_count, local_length, QUERY_HEADS, HEAD_DIM
    )
    key_rows = float_product(normed_input, full_key_weight).reshape(
        sequence_count, local_length, KEY_VALUE_HEADS, HEAD_DIM
    )
    value_rows = (
        float_product(normed_input, full_value_weight)
        .astype(jnp.bfloat16)
        .reshape(sequence_count, local_length, KEY_VALUE_HEADS, HEAD_DIM)
    )
    q_scale = rms_scale(query)
    key_scale = rms_scale(key_rows)
    cosine, sine = rope_tables(local_pos)
    query_rotated = rotate(query * q_scale * g_query, cosine, sine).astype(jnp.bfloat16)
    k_rot = rotate(key_rows * key_scale * key_gain, cosine, sine).astype(jnp.bfloat16)
    keys_all, values_all = (
        lax.all_gather(k_rot, "ctx", axis=1, tiled=True),
        lax.all_gather(value_rows, "ctx", axis=1, tiled=True),
    )
    allowed = (
        (local_seg[:, :, None] == segments[:, None, :])
        & (positions[:, None, :] <= local_pos[:, :, None])
    )[:, None, None]
    query_group = query_rotated.reshape(
        sequence_count, local_length, KEY_VALUE_HEADS, group_width, HEAD_DIM
    )
    scores = (
        jnp.einsum("bqkgd,bskd->bkgqs", query_group, keys_all, preferred_element_type=jnp.float32)
        * score_scale
    )
    exponent = jnp.where(allowed, jnp.exp(scores), 0.0)
    denominator = jnp.sum(exponent, axis=-1)
    log_total = jnp.log(denominator)
    probs = (exponent / denominator[..., None]).astype(jnp.bfloat16)
    attention_output = jnp.einsum(
        "bkgqs,bskd->bqkgd", probs, values_all, preferred_element_type=jnp.float32
    )
    attention_output = attention_output.astype(jnp.bfloat16).reshape(
        total_rows, QUERY_HEADS * HEAD_DIM
    )
    mixed_in = x_rows + float_product(attention_output, wo_full)
    scale_mid = rms_scale(mixed_in)
    normed_mid = (mixed_in * scale_mid * g_mlp).astype(jnp.bfloat16)
    wg_full, wu_full, wd_full = (
        lax.all_gather(w_gate, ("shard", "ctx"), axis=1, tiled=True),
        lax.all_gather(w_up, ("shard", "ctx"), axis=1, tiled=True),
        lax.all_gather(w_down, ("shard", "ctx"), axis=0, tiled=True),
    )
    gate_pre = float_product(normed_mid, wg_full)
    up_pre = float_product(normed_mid, wu_full)
    sigmoid_gate = jax.nn.sigmoid(gate_pre)
    hidden = (gate_pre * sigmoid_gate * up_pre).astype(jnp.bfloat16)
    block_sum = mixed_in + float_product(hidden, wd_full)
    block_out = block_sum.astype(jnp.bfloat16).reshape(sequence_count, local_length, model_width)
    grad_rows = cotangent.reshape(total_rows, model_width)
    d_hidden = against_rows(grad_rows, wd_full)
    grad_down = over_tokens(hidden, grad_rows)
    d_gate = (d_hidden * up_pre * sigmoid_gate * (1.0 + gate_pre * (1.0 - sigmoid_gate))).astype(
        jnp.bfloat16
    )
    d_up = (d_hidden * gate_pre * sigmoid_gate).astype(jnp.bfloat16)
    grad_gate = over_tokens(normed_mid, d_gate)
    grad_up = over_tokens(normed_mid, d_up)
    owned_gate, owned_up, owned_down = (
        lax.psum_scatter(grad_gate, ("shard", "ctx"), scatter_dimension=1, tiled=True),
        lax.psum_scatter(grad_up, ("shard", "ctx"), scatter_dimension=1, tiled=True),
        lax.psum_scatter(grad_down, ("shard", "ctx"), scatter_dimension=0, tiled=True),
    )
    total_gate, total_up, total_down = (
        lax.psum(owned_gate.astype(jnp.bfloat16), "rep").astype(jnp.float32),
        lax.psum(owned_up.astype(jnp.bfloat16), "rep").astype(jnp.float32),
        lax.psum(owned_down.astype(jnp.bfloat16), "rep").astype(jnp.float32),
    )
    d_mid = against_rows(d_gate, wg_full) + against_rows(d_up, wu_full)
    dg_mlp = jnp.sum(d_mid * mixed_in * scale_mid, axis=0)
    d_resid = grad_rows.astype(jnp.float32) + norm_backward(d_mid, mixed_in, scale_mid, g_mlp)
    residual_gradient_bfloat = d_resid.astype(jnp.bfloat16)
    grad_output = over_tokens(attention_output, residual_gradient_bfloat)
    attention_gradient = (
        against_rows(residual_gradient_bfloat, wo_full)
        .astype(jnp.bfloat16)
        .reshape(sequence_count, local_length, KEY_VALUE_HEADS, group_width, HEAD_DIM)
    )
    attention_heads = attention_output.reshape(
        sequence_count, local_length, KEY_VALUE_HEADS, group_width, HEAD_DIM
    )
    row_delta = jnp.sum(
        attention_gradient.astype(jnp.float32) * attention_heads.astype(jnp.float32), axis=-1
    )
    row_delta = jnp.transpose(row_delta, (0, 2, 3, 1))
    scores_again = (
        jnp.einsum("bqkgd,bskd->bkgqs", query_group, keys_all, preferred_element_type=jnp.float32)
        * score_scale
    )
    probs_back = jnp.where(allowed, jnp.exp(scores_again - log_total[..., None]), 0.0)
    probs_round = probs_back.astype(jnp.bfloat16)
    values_gradient = jnp.einsum(
        "bkgqs,bqkgd->bskd", probs_round, attention_gradient, preferred_element_type=jnp.float32
    )
    d_probs = jnp.einsum(
        "bqkgd,bskd->bkgqs", attention_gradient, values_all, preferred_element_type=jnp.float32
    )
    d_scores = (probs_back * (d_probs - row_delta[..., None])).astype(jnp.bfloat16)
    d_qrot = (
        jnp.einsum("bkgqs,bskd->bqkgd", d_scores, keys_all, preferred_element_type=jnp.float32)
        * score_scale
    )
    d_krot = (
        jnp.einsum("bkgqs,bqkgd->bskd", d_scores, query_group, preferred_element_type=jnp.float32)
        * score_scale
    )
    d_keys, value_rows_gradient = (
        lax.psum_scatter(
            d_krot.astype(jnp.bfloat16), "ctx", scatter_dimension=1, tiled=True
        ).astype(jnp.float32),
        lax.psum_scatter(
            values_gradient.astype(jnp.bfloat16), "ctx", scatter_dimension=1, tiled=True
        ).astype(jnp.float32),
    )
    d_qn = rotate_back(
        d_qrot.reshape(sequence_count, local_length, QUERY_HEADS, HEAD_DIM), cosine, sine
    )
    normed_key_gradient = rotate_back(d_keys, cosine, sine)
    dg_query = jnp.sum(d_qn * query * q_scale, axis=(0, 1, 2))
    dg_key = jnp.sum(normed_key_gradient * key_rows * key_scale, axis=(0, 1, 2))
    d_query = (
        norm_backward(d_qn, query, q_scale, g_query)
        .astype(jnp.bfloat16)
        .reshape(total_rows, QUERY_HEADS * HEAD_DIM)
    )
    key_gradient = (
        norm_backward(normed_key_gradient, key_rows, key_scale, key_gain)
        .astype(jnp.bfloat16)
        .reshape(total_rows, KEY_VALUE_HEADS * HEAD_DIM)
    )
    value_gradient = value_rows_gradient.astype(jnp.bfloat16).reshape(
        total_rows, KEY_VALUE_HEADS * HEAD_DIM
    )
    grad_query = over_tokens(normed_input, d_query)
    grad_key = over_tokens(normed_input, key_gradient)
    grad_value = over_tokens(normed_input, value_gradient)
    d_in = (
        against_rows(d_query, wq_full)
        + against_rows(key_gradient, full_key_weight)
        + against_rows(value_gradient, full_value_weight)
    )
    dg_attn = jnp.sum(d_in * x_rows * scale_in, axis=0)
    grad_input = (d_resid + norm_backward(d_in, x_rows, scale_in, g_attn)).reshape(
        sequence_count, local_length, model_width
    )
    grad_gains = jnp.concatenate([dg_attn, dg_query, dg_key, dg_mlp])
    owned_query, owned_key, owned_value, owned_output, owned_gains = (
        lax.psum_scatter(grad_query, ("shard", "ctx"), scatter_dimension=1, tiled=True),
        lax.psum_scatter(grad_key, ("shard", "ctx"), scatter_dimension=1, tiled=True),
        lax.psum_scatter(grad_value, ("shard", "ctx"), scatter_dimension=1, tiled=True),
        lax.psum_scatter(grad_output, ("shard", "ctx"), scatter_dimension=0, tiled=True),
        lax.psum_scatter(grad_gains, ("shard", "ctx"), scatter_dimension=0, tiled=True),
    )
    total_query, total_key, total_value, total_output, total_gains = (
        lax.psum(owned_query.astype(jnp.bfloat16), "rep").astype(jnp.float32),
        lax.psum(owned_key.astype(jnp.bfloat16), "rep").astype(jnp.float32),
        lax.psum(owned_value.astype(jnp.bfloat16), "rep").astype(jnp.float32),
        lax.psum(owned_output.astype(jnp.bfloat16), "rep").astype(jnp.float32),
        lax.psum(owned_gains.astype(jnp.bfloat16), "rep").astype(jnp.float32),
    )
    return (
        block_out,
        grad_input,
        total_query,
        total_key,
        total_value,
        total_output,
        total_gate,
        total_up,
        total_down,
        total_gains,
    )


def row_plan(head_half, ff):
    sizes = (
        ("q", HEAD_DIM, HEAD_DIM),
        ("k", head_half, HEAD_DIM),
        ("v", head_half, HEAD_DIM),
        ("o", HEAD_DIM, HEAD_DIM),
        ("g", ff, ff),
        ("u", ff, ff),
        ("d", ff, ff),
    )
    plan, own, full = {}, 0, 0
    for name, own_rows, block_rows in sizes:
        plan[name] = (own, own_rows, full, block_rows)
        own, full = own + own_rows, full + 4 * block_rows
    return plan, own, full


def plain(left, right):
    return lax.dot_general(left, right, (((1,), (0,)), ((), ())), preferred_element_type=jnp.float32)


def swap_halves(values_in):
    return pltpu.roll(values_in, values_in.shape[-1] // 2, 1)


def rows(start, size, step):
    return pl.ds(pl.multiple_of(start, step), size)


def layer_kernel(
    plan,
    tok,
    cot,
    wst,
    gain_in,
    mask,
    cosine,
    sine,
    block_out,
    grad_in,
    grad_w,
    gain_out,
    x_all,
    c_all,
    nx,
    nm,
    res,
    own_mid,
    own_res,
    wb,
    qf,
    kf,
    qr,
    kr,
    vb,
    prob,
    att,
    hid,
    dga,
    dup,
    dqb,
    dkb,
    dvb,
    mixed,
    dres,
    part_a,
    part_b,
    got_a,
    got_b,
    got_c,
    got_d,
    gz,
    gsum,
    gz_s,
    gfull,
    dgt,
    dz,
    dsum,
    dz_s,
    dtot,
    dz_x,
    gb,
    rk,
    hs,
    ry,
    kvh,
    kvr,
    xo,
    rx,
    send_sem,
    recv_sem,
):
    sequences, span, width = tok.shape
    ctx = lax.axis_size("ctx")
    length = span * ctx
    heads = 4
    scale = 1.0 / math.sqrt(HEAD_DIM)
    r, s, c = lax.axis_index("rep"), lax.axis_index("shard"), lax.axis_index("ctx")
    core, side = s % 2, s // 2
    sib, opp = s + 1 - 2 * core, (s + 2) % 4
    dia = (sib + 2) % 4
    mine, theirs = core * 2 + side, core * 2 + 1 - side
    half = c % 2
    partner = c + 1 - 2 * half
    steps = list(range(1, ctx))
    sends = []

    def send(src, dst, **where):
        at = len(sends)
        copy = pltpu.make_async_remote_copy(
            src_ref=src,
            dst_ref=dst,
            send_sem=send_sem.at[at],
            recv_sem=recv_sem.at[at],
            device_id=where,
            device_id_type=MESH,
        )
        copy.start()
        sends.append(copy)
        return copy

    def arrive(copies):
        for copy in copies:
            copy.wait_recv()

    def around(d):
        return lax.rem(c + d, ctx)

    def gather(src, dst):
        return [send(src, dst.at[:, c], ctx=around(d)) for d in steps]

    def scatter(src, dst):
        return [send(src.at[around(d)], dst.at[d - 1], ctx=around(d)) for d in steps]

    def keep(src, dst):
        for b in range(sequences):
            dst[b, c] = src[b]

    def block(name, at):
        _, _, off, size = plan[name]
        return rows(off + at * size, size, 64)

    def spread(name, src):
        own = block(name, mine)
        return send(src, wb.at[own], shard=opp), send(src, wb.at[own], shard=sib)

    def pass_on(name):
        got = block(name, theirs)
        return send(wb.at[got], wb.at[got], shard=sib)

    def own_rows(name):
        off, size = plan[name][:2]
        return pl.ds(off, size)

    def matrix(name):
        _, _, off, size = plan[name]
        return wb[pl.ds(off, 4 * size), :]

    def whole(ref, b):
        return ref[b].reshape(length, width)

    def split(values_in, dst, b):
        for j in range(ctx):
            dst[j, b] = values_in[j * span : (j + 1) * span].astype(jnp.bfloat16)

    def collect(src, got, b):
        total = src[c, b].astype(jnp.float32)
        for d in steps:
            total = total + got[d - 1, b].astype(jnp.float32)
        return total

    barrier = pltpu.get_barrier_semaphore()
    peers = [{"ctx": around(d)} for d in steps]
    peers += [{"shard": sib}, {"shard": opp}, {"shard": dia}, {"rep": 1 - r}]
    for peer in peers:
        pl.semaphore_signal(barrier, inc=1, device_id=peer, device_id_type=MESH)
    pl.semaphore_wait(barrier, len(peers))

    head_half = plan["k"][1]
    lanes = [
        rows(plan[name][2] + mine * HEAD_DIM + half * head_half, head_half, 64) for name in "kv"
    ]
    kv_in = [send(wst.at[own_rows(n)], wb.at[at], ctx=partner) for n, at in zip("kv", lanes)]
    gains = [send(gain_in, gz.at[d - 1], ctx=around(d)) for d in steps]
    tok_in = gather(tok, x_all)
    spreads = {"q": spread("q", wst.at[own_rows("q")])}
    for n, at in zip("kv", lanes):
        wb[at, :] = wst[own_rows(n), :]
    for n in "qogud":
        wb[block(n, mine), :] = wst[own_rows(n), :]
    keep(tok, x_all)
    keep(cot, c_all)
    arrive(kv_in)
    for n in "kv":
        spreads[n] = spread(n, wb.at[block(n, mine)])
    for n in "ogud":
        spreads[n] = spread(n, wst.at[own_rows(n)])
    arrive(gains)
    total = gain_in[...]
    for d in steps:
        total = total + gz[d - 1]
    gsum[...] = total
    gains = [send(gsum, gz_s.at[i], shard=p) for i, p in enumerate((sib, opp, dia))]
    arrive(tok_in)
    cot_in = gather(cot, c_all)
    arrive(gains)
    gfull[...] = gsum[...] + gz_s[0] + gz_s[1] + gz_s[2]
    g_attn = gfull[0:1, :]
    g_mlp = gfull[1:2, :]
    g_query = gfull[2:3, :HEAD_DIM]
    g_key = gfull[2:3, HEAD_DIM : 2 * HEAD_DIM]

    def norm_rows(i, carry):
        b, j = i // ctx, i % ctx
        x = x_all[b, j].astype(jnp.float32)
        nx[b, j] = (x * rms_scale(x) * g_attn).astype(jnp.bfloat16)
        return carry

    lax.fori_loop(0, sequences * ctx, norm_rows, 0)

    passed = {}
    for n in "qkv":
        arrive([spreads[n][0]])
        passed[n] = pass_on(n)
    for n in "qkv":
        arrive([spreads[n][1], passed[n]])

    def attend(b, carry):
        x = whole(nx, b)
        query = against_rows(x, matrix("q"))
        key = against_rows(x, matrix("k"))
        value = against_rows(x, matrix("v")).astype(jnp.bfloat16)
        cos_b, sin_b, allowed = cosine[b], sine[b], mask[b] > 0.5
        for h in range(heads):
            at = slice(h * HEAD_DIM, (h + 1) * HEAD_DIM)
            q, k, v = query[:, at], key[:, at], value[:, at]
            qn = q * rms_scale(q) * g_query
            kn = k * rms_scale(k) * g_key
            q_rot = (qn * cos_b + swap_halves(qn) * sin_b).astype(jnp.bfloat16)
            k_rot = (kn * cos_b + swap_halves(kn) * sin_b).astype(jnp.bfloat16)
            qf[b, h], kf[b, h] = q, k
            qr[b, h], kr[b, h], vb[b, h] = q_rot, k_rot, v
            scores = against_rows(q_rot, k_rot) * scale
            exponent = jnp.where(allowed, jnp.exp(scores), 0.0)
            p = exponent / jnp.sum(exponent, axis=-1, keepdims=True)
            prob[b, h] = p
            att[b, :, at] = plain(p.astype(jnp.bfloat16), v).astype(jnp.bfloat16)
        return carry

    lax.fori_loop(0, sequences, attend, 0)

    arrive([spreads["o"][0]])
    passed["o"] = pass_on("o")
    arrive([spreads["o"][1], passed["o"]])

    def project(b, carry):
        split(plain(att[b], matrix("o")), part_a, b)
        return carry

    lax.fori_loop(0, sequences, project, 0)
    copies = scatter(part_a, got_a)
    for n in "gud":
        arrive([spreads[n][0]])
        passed[n] = pass_on(n)
    arrive(copies)
    for b in range(sequences):
        m = tok[b].astype(jnp.float32) + collect(part_a, got_a, b)
        mixed[b] = m
        own_mid[b] = (m * rms_scale(m) * g_mlp).astype(jnp.bfloat16)
    mid_in = gather(own_mid, nm)
    keep(own_mid, nm)
    for n in "gud":
        arrive([spreads[n][1], passed[n]])
    arrive(cot_in)
    arrive(mid_in)

    def feed(b, carry):
        n, ct = whole(nm, b), whole(c_all, b)
        gate = against_rows(n, matrix("g"))
        up = against_rows(n, matrix("u"))
        d_hidden = against_rows(ct, matrix("d"))
        sig = jax.nn.sigmoid(gate)
        hid[b] = (gate * sig * up).astype(jnp.bfloat16)
        d_gate = (d_hidden * up * sig * (1.0 + gate * (1.0 - sig))).astype(jnp.bfloat16)
        d_up = (d_hidden * gate * sig).astype(jnp.bfloat16)
        dga[b], dup[b] = d_gate, d_up
        split(plain(d_gate, matrix("g")) + plain(d_up, matrix("u")), part_b, b)
        return carry

    lax.fori_loop(0, sequences, feed, 0)
    mid_back = scatter(part_b, got_b)
    for copy in copies:
        copy.wait_send()

    def leave(b, carry):
        split(plain(hid[b], matrix("d")), part_a, b)
        return carry

    lax.fori_loop(0, sequences, leave, 0)
    out_back = scatter(part_a, got_c)

    def flat(ref):
        return ref.reshape(sequences * length, ref.shape[-1])

    def weigh(name, left, right):
        _, _, off, size = plan[name]
        right = right[...].reshape(sequences * length, width)
        chunk = 256

        def some(i, carry):
            at = pl.multiple_of(i * chunk, chunk)
            lhs = left[:, :, pl.ds(at, chunk)].reshape(sequences * length, chunk)
            gb[rows(off + at, chunk, 64), :] = over_tokens(lhs, right).astype(jnp.bfloat16)
            return carry

        lax.fori_loop(0, 4 * size // chunk, some, 0)
        return send(
            gb.at[rows(off + (1 - core) * 2 * size, 2 * size, 64)],
            rk.at[pl.ds(off // 2, 2 * size)],
            shard=sib,
        )

    def drain_core(name, copy):
        _, _, off, size = plan[name]
        arrive([copy])
        here = rows(off + theirs * size, size, 64)
        there = rows(off // 2 + (1 - side) * size, size, 64)
        total = gb[here, :].astype(jnp.float32) + rk[there, :].astype(jnp.float32)
        at = pl.ds(off // 4, size)
        hs[at, :] = total.astype(jnp.bfloat16)
        return send(hs.at[at], ry.at[at], shard=opp)

    def drain_side(name, copy):
        own, own_size, off, size = plan[name]
        arrive([copy])
        here = rows(off + mine * size, size, 64)
        there = rows(off // 2 + side * size, size, 64)
        total = gb[here, :].astype(jnp.float32) + rk[there, :].astype(jnp.float32)
        total = total + ry[pl.ds(off // 4, size), :].astype(jnp.float32)
        total = total.astype(jnp.bfloat16)
        at = pl.ds(own, own_size)
        if own_size == size:
            xo[at, :] = total
            return send(xo.at[at], rx.at[at], rep=1 - r)
        i = "kv".index(name)
        kvh[i] = total
        return send(kvh.at[i, rows((1 - half) * own_size, own_size, 64)], kvr.at[i], ctx=partner)

    def drain_pair(name, copy):
        own, own_size, _, _ = plan[name]
        arrive([copy])
        i = "kv".index(name)
        total = kvh[i, rows(half * own_size, own_size, 64), :].astype(jnp.float32)
        at = pl.ds(own, own_size)
        xo[at, :] = (total + kvr[i].astype(jnp.float32)).astype(jnp.bfloat16)
        return send(xo.at[at], rx.at[at], rep=1 - r)

    def drain_rep(name, copy):
        at = own_rows(name)
        arrive([copy])
        grad_w[at, :] = xo[at, :].astype(jnp.float32) + rx[at, :].astype(jnp.float32)

    moving = {}
    moving["d"] = weigh("d", hid, c_all)
    moving["g"] = weigh("g", dga, nm)
    moving["u"] = weigh("u", dup, nm)

    dgt[...] = jnp.zeros_like(dgt)
    arrive(mid_back)
    for b in range(sequences):
        d_mid = collect(part_b, got_b, b)
        m = mixed[b]
        r_mid = rms_scale(m)
        dgt[1:2, :] += jnp.sum(d_mid * m * r_mid, axis=0, keepdims=True)
        d_resid = cot[b].astype(jnp.float32) + norm_backward(d_mid, m, r_mid, g_mlp)
        dres[b] = d_resid
        own_res[b] = d_resid.astype(jnp.bfloat16)
    res_in = gather(own_res, res)
    keep(own_res, res)
    for n in "dgu":
        moving[n] = drain_core(n, moving[n])
    arrive(out_back)
    for b in range(sequences):
        block_out[b] = (mixed[b] + collect(part_a, got_c, b)).astype(jnp.bfloat16)
    for copy in mid_back:
        copy.wait_send()
    arrive(res_in)
    moving["o"] = weigh("o", att, res)

    def attend_back(b, carry):
        d_att = against_rows(whole(res, b), matrix("o")).astype(jnp.bfloat16)
        cos_b, sin_b = cosine[b], sine[b]

        def through(d_rot, u, gain):
            d_n = d_rot * cos_b - swap_halves(d_rot) * sin_b
            u_scale = rms_scale(u)
            gain_row = jnp.sum(d_n * u * u_scale, axis=0, keepdims=True)
            return norm_backward(d_n, u, u_scale, gain).astype(jnp.bfloat16), gain_row

        for h in range(heads):
            at = slice(h * HEAD_DIM, (h + 1) * HEAD_DIM)
            da, p = d_att[:, at], prob[b, h]
            delta = jnp.sum(
                da.astype(jnp.float32) * att[b, :, at].astype(jnp.float32), axis=-1, keepdims=True
            )
            dvb[b, :, at] = over_tokens(p.astype(jnp.bfloat16), da).astype(jnp.bfloat16)
            d_p = against_rows(da, vb[b, h])
            d_s = (p * (d_p - delta)).astype(jnp.bfloat16)
            d_q, row_q = through(plain(d_s, kr[b, h]) * scale, qf[b, h], g_query)
            d_k, row_k = through(over_tokens(d_s, qr[b, h]) * scale, kf[b, h], g_key)
            dqb[b, :, at] = d_q
            dkb[b, :, at] = d_k
            dgt[2:3, :HEAD_DIM] += row_q
            dgt[2:3, HEAD_DIM : 2 * HEAD_DIM] += row_k
        d_in = plain(dqb[b], matrix("q")) + plain(dkb[b], matrix("k")) + plain(dvb[b], matrix("v"))
        split(d_in, part_b, b)
        return carry

    lax.fori_loop(0, sequences, attend_back, 0)
    in_back = scatter(part_b, got_d)
    moving["q"] = weigh("q", dqb, nx)
    moving["k"] = weigh("k", dkb, nx)
    moving["v"] = weigh("v", dvb, nx)
    for n in "dgu":
        moving[n] = drain_side(n, moving[n])
    for n in "okvq":
        moving[n] = drain_core(n, moving[n])
    arrive(in_back)
    for b in range(sequences):
        d_in = collect(part_b, got_d, b)
        x = tok[b].astype(jnp.float32)
        r_in = rms_scale(x)
        dgt[0:1, :] += jnp.sum(d_in * x * r_in, axis=0, keepdims=True)
        grad_in[b] = dres[b] + norm_backward(d_in, x, r_in, g_attn)
    gains = [send(dgt, dz.at[d - 1], ctx=around(d)) for d in steps]
    for n in "okv":
        moving[n] = drain_side(n, moving[n])
    arrive(gains)
    total = dgt[...]
    for d in steps:
        total = total + dz[d - 1]
    dsum[...] = total
    gains = [send(dsum, dz_s.at[i], shard=p) for i, p in enumerate((sib, opp, dia))]
    moving["q"] = drain_side("q", moving["q"])
    for n in "dgu":
        drain_rep(n, moving[n])
    arrive(gains)
    dtot[...] = dsum[...] + dz_s[0] + dz_s[1] + dz_s[2]
    gains = [send(dtot, dz_x, rep=1 - r)]
    for n in "kv":
        moving[n] = drain_pair(n, moving[n])
    for n in "oqkv":
        drain_rep(n, moving[n])
    arrive(gains)
    gain_out[...] = dtot[...] + dz_x[...]
    waited = {id(copy) for copy in copies + mid_back}
    for copy in sends:
        if id(copy) not in waited:
            copy.wait_send()


def whole_layer_body(
    tokens,
    positions,
    segments,
    cotangent,
    w_query,
    key_weight,
    value_weight,
    output_weight,
    w_gate,
    w_up,
    w_down,
    norm_gains,
):
    sequences, span, width = tokens.shape
    ctx = lax.axis_size("ctx")
    length = span * ctx
    ff = w_gate.shape[1]
    half = key_weight.shape[1]
    plan, own_total, full_total = row_plan(half, ff)
    heads = 4
    stacked = jnp.concatenate(
        [
            w_query.T,
            key_weight.T,
            value_weight.T,
            output_weight,
            w_gate.T,
            w_up.T,
            w_down,
        ],
        axis=0,
    )
    count = norm_gains.shape[0]
    place = lax.axis_index("shard") * ctx + lax.axis_index("ctx")
    all_gains = width * 2 + 2 * HEAD_DIM
    spread_gains = lax.dynamic_update_slice(
        jnp.zeros((all_gains,), jnp.float32), norm_gains.astype(jnp.float32), (place * count,)
    )
    gain_rows = jnp.concatenate(
        [
            spread_gains[:width],
            spread_gains[width + 2 * HEAD_DIM :],
            spread_gains[width : width + 2 * HEAD_DIM],
            jnp.zeros((6 * width - 2 * HEAD_DIM,), jnp.float32),
        ]
    ).reshape(8, width)
    cosine, sine = rope_tables(positions)
    cosine, sine = cosine[:, :, 0], sine[:, :, 0]
    cosine = jnp.concatenate([cosine, cosine], axis=-1)
    sine = jnp.concatenate([-sine, sine], axis=-1)
    allowed = (
        (segments[:, :, None] == segments[:, None, :])
        & (positions[:, None, :] <= positions[:, :, None])
    ).astype(jnp.float32)

    bf, f32 = jnp.bfloat16, jnp.float32
    gathered = pltpu.VMEM((sequences, ctx, span, width), bf)
    own_block = pltpu.VMEM((sequences, span, width), bf)
    own_float = pltpu.VMEM((sequences, span, width), f32)
    head_float = pltpu.VMEM((sequences, heads, length, HEAD_DIM), f32)
    head_half = pltpu.VMEM((sequences, heads, length, HEAD_DIM), bf)
    head_lanes = pltpu.VMEM((sequences, length, heads * HEAD_DIM), bf)
    ff_lanes = pltpu.VMEM((sequences, length, heads * ff), bf)
    parts = pltpu.VMEM((ctx, sequences, span, width), bf)
    got = pltpu.VMEM((ctx - 1, sequences, span, width), bf)
    tile = pltpu.VMEM((8, width), f32)
    tiles_c = pltpu.VMEM((ctx - 1, 8, width), f32)
    tiles_s = pltpu.VMEM((3, 8, width), f32)

    def row_buffer(n):
        return pltpu.VMEM((n, width), bf)

    copies = 128
    vmem = pl.BlockSpec(memory_space=pltpu.VMEM)
    block_out, grad_input, grads, gains_sum = pl.pallas_call(
        functools.partial(layer_kernel, plan),
        out_shape=(
            jax.ShapeDtypeStruct(tokens.shape, bf),
            jax.ShapeDtypeStruct(tokens.shape, f32),
            jax.ShapeDtypeStruct((own_total, width), f32),
            jax.ShapeDtypeStruct((8, width), f32),
        ),
        in_specs=[vmem] * 7,
        out_specs=[vmem] * 4,
        scratch_shapes=[
            gathered,
            gathered,
            gathered,
            gathered,
            gathered,
            own_block,
            own_block,
            row_buffer(full_total),
            head_float,
            head_float,
            head_half,
            head_half,
            head_half,
            pltpu.VMEM((sequences, heads, length, length), f32),
            head_lanes,
            ff_lanes,
            ff_lanes,
            ff_lanes,
            head_lanes,
            head_lanes,
            head_lanes,
            own_float,
            own_float,
            parts,
            parts,
            got,
            got,
            got,
            got,
            tiles_c,
            tile,
            tiles_s,
            tile,
            tile,
            tiles_c,
            tile,
            tiles_s,
            tile,
            tile,
            row_buffer(full_total),
            row_buffer(full_total // 2),
            row_buffer(full_total // 4),
            row_buffer(full_total // 4),
            pltpu.VMEM((2, HEAD_DIM, width), bf),
            pltpu.VMEM((2, half, width), bf),
            row_buffer(own_total),
            row_buffer(own_total),
            pltpu.SemaphoreType.DMA((copies,)),
            pltpu.SemaphoreType.DMA((copies,)),
        ],
        compiler_params=pltpu.CompilerParams(
            collective_id=0, has_side_effects=True, vmem_limit_bytes=67043328
        ),
    )(tokens, cotangent, stacked, gain_rows, allowed, cosine, sine)

    def part(name):
        at, size = plan[name][:2]
        return grads[at : at + size]

    flat = jnp.concatenate([gains_sum[0], gains_sum[2, : 2 * HEAD_DIM], gains_sum[1]])
    return (
        block_out,
        grad_input,
        part("q").T,
        part("k").T,
        part("v").T,
        part("o"),
        part("g").T,
        part("u").T,
        part("d"),
        lax.dynamic_slice(flat, (place * count,), (count,)),
    )


def any_body(*arguments):
    tokens, w_query, key_weight, w_gate = (arguments[i] for i in (0, 4, 5, 8))
    ctx, shards = lax.axis_size("ctx"), lax.axis_size("shard")
    fits = w_query.shape[1] == HEAD_DIM and 2 * key_weight.shape[1] == HEAD_DIM
    fits = fits and lax.axis_size("rep") == 2 and shards == 4 and ctx % 2 == 0
    fits = fits and w_gate.shape[1] % 64 == 0 and tokens.shape[1] % 16 == 0
    fits = fits and tokens.shape[0] * tokens.shape[1] * ctx <= 512
    if fits:
        return whole_layer_body(*arguments)
    return body(*arguments)


def solution(mesh):
    in_specs = (
        P(("rep", "shard"), "ctx", None),
        P(("rep", "shard"), None),
        P(("rep", "shard"), None),
        P(("rep", "shard"), "ctx", None),
        P(None, ("shard", "ctx")),
        P(None, ("shard", "ctx")),
        P(None, ("shard", "ctx")),
        P(("shard", "ctx"), None),
        P(None, ("shard", "ctx")),
        P(None, ("shard", "ctx")),
        P(("shard", "ctx"), None),
        P(("shard", "ctx")),
    )
    out_specs = (
        P(("rep", "shard"), "ctx", None),
        P(("rep", "shard"), "ctx", None),
        P(None, ("shard", "ctx")),
        P(None, ("shard", "ctx")),
        P(None, ("shard", "ctx")),
        P(("shard", "ctx"), None),
        P(None, ("shard", "ctx")),
        P(None, ("shard", "ctx")),
        P(("shard", "ctx"), None),
        P(("shard", "ctx")),
    )
    return jax.shard_map(any_body, mesh=mesh, in_specs=in_specs, out_specs=out_specs, check_vma=False)
```

profile of v0, /device:TPU:0, one launch (start us, length us, event | category | flops | bytes accessed | tf_op | source)
XLA Modules:
  0.0 273.7 jit_solution(7376430718959964849)
XLA Ops:
  0.6 0.0 copy-start.6
  0.7 0.7 convert_element_type.11
  1.4 0.7 convert_dynamic-update-slice_fusion
  2.2 0.6 reshape.34.gain_in
  2.8 0.0 copy-start.7
  2.8 1.1 copy.22
  3.9 0.0 copy-start.4
  3.9 1.8 and_convert_fusion.mask
  5.7 0.0 copy-start.1
  5.7 1.0 fusion
  6.7 0.0 copy-start.2
  6.7 0.0 copy-start.3
  6.7 1.0 pad_maximum_fusion
  7.7 0.7 bitcast_dynamic-update-slice_fusion.2
  8.4 0.0 copy-done.6
  8.4 0.7 bitcast_dynamic-update-slice_fusion.4
  9.1 0.0 copy-done.7
  9.1 0.7 bitcast_dynamic-update-slice_fusion.3
  9.8 0.0 copy-done.4
  9.8 0.7 constant_dynamic-update-slice_fusion.1
  10.5 0.0 copy-done.1
  10.5 0.8 bitcast_dynamic-update-slice_fusion.1
  11.3 0.0 copy-done.2
  11.3 0.8 bitcast_dynamic-update-slice_fusion
  12.1 0.0 copy-done.3
  12.1 0.8 constant_dynamic-update-slice_fusion.wst
  12.8 249.0 %shard_map.195 = (bf16[2,64,1024]{2,1,0:T(8,128)(2,1)}, f32[2,64,1024]{2,1,0:T(8,128)}, f32[960,1024]{1,0:T(8,128)}, f32[8,1024]{1,0:T(8,128)}) custom-call(bf16[2,64,1024]{2,1,0:T(8,128)(2,1)} %tok.1, bf16[2,64,1024]{2,1,0:T(8,128)(2,1)} %cot.1, bf16[960,1024]{1,0:T(8,128)(2,1)} %constant_dynamic-update-slice_fusion.wst, f32[8,1024]{1,0:T(8,128)} %reshape.34.gain_in, ...), custom_call_target="tpu_custom_call" | custom-call | tf_op jit(solution)/shard_map/pallas_call | solution.py:824
  261.9 0.7 slice.50
  262.6 0.8 fusion.5
  263.4 0.6 fusion.2
  264.1 1.9 slice_bitcast_fusion.3
  265.9 2.1 fusion.4
  268.0 0.0 copy-start.5
  268.0 0.0 copy-start
  268.0 3.2 %fusion.3 = (f32[192,1024]{1,0:T(8,128)}, f32[1024,192]{0,1:T(8,128)}, f32[1024,192]{0,1:T(8,128)}) fusion(f32[960,1024]{1,0:T(8,128)} %get-tuple-element.16), kind=kLoop, calls=%fused_computation.26 | loop fusion | bytes 4718592 | tf_op jit(solution)/shard_map/slice | solution.py:892
  271.2 1.0 copy.23
  272.2 0.0 copy-done.5
  272.2 0.7 copy.33
  272.9 0.0 copy-done
  272.9 0.8 copy.34
  (6 shorter events, 0.0 us)
Async XLA Ops:
  0.6 7.8 %copy-start.6 = (bf16[1024,64]{0,1:T(8,128)(2,1)S(1)}, bf16[1024,64]{0,1:T(8,128)(2,1)}, u32[]{:S(2)}) copy-start(bf16[1024,64]{0,1:T(8,128)(2,1)} %param.17) | copy-start | bytes 393220
  2.8 6.3 %copy-start.7 = (bf16[1024,64]{0,1:T(8,128)(2,1)S(1)}, bf16[1024,64]{0,1:T(8,128)(2,1)}, u32[]{:S(2)}) copy-start(bf16[1024,64]{0,1:T(8,128)(2,1)} %param.18) | copy-start | bytes 393220
  3.9 5.8 %copy-start.4 = (bf16[128,1024]{1,0:T(8,128)(2,1)S(1)}, bf16[128,1024]{1,0:T(8,128)(2,1)}, u32[]{:S(2)}) copy-start(bf16[128,1024]{1,0:T(8,128)(2,1)} %param.19) | copy-start | bytes 786436
  5.7 4.8 %copy-start.1 = (bf16[1024,192]{0,1:T(8,128)(2,1)S(1)}, bf16[1024,192]{0,1:T(8,128)(2,1)}, u32[]{:S(2)}) copy-start(bf16[1024,192]{0,1:T(8,128)(2,1)} %param.20) | copy-start | bytes 1179652
  6.7 4.6 %copy-start.2 = (bf16[1024,192]{0,1:T(8,128)(2,1)S(1)}, bf16[1024,192]{0,1:T(8,128)(2,1)}, u32[]{:S(2)}) copy-start(bf16[1024,192]{0,1:T(8,128)(2,1)} %param.21) | copy-start | bytes 1179652
  6.7 5.3 %copy-start.3 = (bf16[192,1024]{1,0:T(8,128)(2,1)S(1)}, bf16[192,1024]{1,0:T(8,128)(2,1)}, u32[]{:S(2)}) copy-start(bf16[192,1024]{1,0:T(8,128)(2,1)} %param.22) | copy-start | bytes 1179652
  268.0 4.2 %copy-start.5 = (bf16[2,64,1024]{2,1,0:T(8,128)(2,1)S(1)}, bf16[2,64,1024]{2,1,0:T(8,128)(2,1)}, u32[]{:S(2)}) copy-start(bf16[2,64,1024]{2,1,0:T(8,128)(2,1)} %get-tuple-element.54) | copy-start | bytes 786436
  268.0 4.9 %copy-start = (f32[2,64,1024]{2,1,0:T(8,128)S(1)}, f32[2,64,1024]{2,1,0:T(8,128)}, u32[]{:S(2)}) copy-start(f32[2,64,1024]{2,1,0:T(8,128)} %get-tuple-element.55) | copy-start | bytes 1572868
where the time goes:
time: 277 us; the launch traced here: 274 us
  Pallas kernels  249 us (90%)
  local copies, waits for them, and re-layouts  18 us (6%)
  other arithmetic  5.88 us (2%)
    pallas_call x1, Pallas kernels, whole_layer_body(): pl.pallas_call(functools.partial(layer_kernel, plan), out_shape=(jax.Shap...  249 us
    unnamed x26, local copies, waits for them, and re-layouts  7.96 us

commit v1 on v0

--- a/solution.py
+++ b/solution.py
@@ -318,14 +318,23 @@
     plan,
     tok,
     cot,
-    wst,
+    columns,
+    out_rows,
+    down_rows,
     gain_in,
-    mask,
+    pos,
+    seg,
     cosine,
     sine,
     block_out,
     grad_in,
-    grad_w,
+    grad_q,
+    grad_k,
+    grad_v,
+    grad_o,
+    grad_g,
+    grad_u,
+    grad_d,
     gain_out,
     x_all,
     c_all,
@@ -334,6 +343,7 @@
     res,
     own_mid,
     own_res,
+    turned,
     wb,
     qf,
     kf,
@@ -388,9 +398,11 @@
     dia = (sib + 2) % 4
     mine, theirs = core * 2 + side, core * 2 + 1 - side
     half = c % 2
-    partner = c + 1 - 2 * half
-    steps = list(range(1, ctx))
-    sends = []
+    near = c + 1 - 2 * half
+    far = (c + 2) % 4
+    other = (near + 2) % 4
+    both = range(sequences)
+    sends, lent, returned = [], [], []
 
     def send(src, dst, **where):
         at = len(sends)
@@ -410,26 +422,50 @@
         for copy in copies:
             copy.wait_recv()
 
-    def around(d):
-        return lax.rem(c + d, ctx)
-
-    def gather(src, dst):
-        return [send(src, dst.at[:, c], ctx=around(d)) for d in steps]
-
-    def scatter(src, dst):
-        return [send(src.at[around(d)], dst.at[d - 1], ctx=around(d)) for d in steps]
-
-    def keep(src, dst):
-        for b in range(sequences):
-            dst[b, c] = src[b]
+    def reclaim(copies):
+        for copy in copies:
+            copy.wait_send()
+            returned.append(copy)
+
+    def gather_start(src, dst, b):
+        dst[b, c] = src[b]
+        across = send(src.at[b], dst.at[b, c], ctx=far)
+        beside = send(src.at[b], dst.at[b, c], ctx=near)
+        return beside, across
+
+    def gather_pass(dst, b, pair):
+        arrive([pair[1]])
+        return pair[0], send(dst.at[b, far], dst.at[b, far], ctx=near)
+
+    def reduce_start(src, got, b):
+        first = send(src.at[other, b], got.at[0, b], ctx=near)
+        second = send(src.at[near, b], got.at[1, b], ctx=near)
+        lent.extend((first, second))
+        return first, second
+
+    def reduce_pass(src, got, b, pair):
+        arrive([pair[0]])
+        total = src[far, b].astype(jnp.float32) + got[0, b].astype(jnp.float32)
+        src[far, b] = total.astype(jnp.bfloat16)
+        third = send(src.at[far, b], got.at[2, b], ctx=far)
+        lent.append(third)
+        return pair[1], third
+
+    def reduce_end(src, got, b, pair):
+        arrive(pair)
+        total = src[c, b].astype(jnp.float32) + got[1, b].astype(jnp.float32)
+        return total + got[2, b].astype(jnp.float32)
 
     def block(name, at):
         _, _, off, size = plan[name]
         return rows(off + at * size, size, 64)
 
-    def spread(name, src):
-        own = block(name, mine)
-        return send(src, wb.at[own], shard=opp), send(src, wb.at[own], shard=sib)
+    def spread_rows(own):
+        there = send(wb.at[own], wb.at[own], shard=opp)
+        return [there], [send(wb.at[own], wb.at[own], shard=sib)]
+
+    def spread(name):
+        return spread_rows(block(name, mine))
 
     def pass_on(name):
         got = block(name, theirs)
@@ -450,74 +486,84 @@
         for j in range(ctx):
             dst[j, b] = values_in[j * span : (j + 1) * span].astype(jnp.bfloat16)
 
-    def collect(src, got, b):
-        total = src[c, b].astype(jnp.float32)
-        for d in steps:
-            total = total + got[d - 1, b].astype(jnp.float32)
-        return total
+    def turn(first):
+        at = pl.ds(first, HEAD_DIM)
+        turned[at, :] = columns[:, at].astype(jnp.float32).T.astype(jnp.bfloat16)
 
     barrier = pltpu.get_barrier_semaphore()
-    peers = [{"ctx": around(d)} for d in steps]
+    peers = [{"ctx": near}, {"ctx": far}, {"ctx": other}]
     peers += [{"shard": sib}, {"shard": opp}, {"shard": dia}, {"rep": 1 - r}]
     for peer in peers:
         pl.semaphore_signal(barrier, inc=1, device_id=peer, device_id_type=MESH)
     pl.semaphore_wait(barrier, len(peers))
 
-    head_half = plan["k"][1]
-    lanes = [
-        rows(plan[name][2] + mine * HEAD_DIM + half * head_half, head_half, 64) for name in "kv"
-    ]
-    kv_in = [send(wst.at[own_rows(n)], wb.at[at], ctx=partner) for n, at in zip("kv", lanes)]
-    gains = [send(gain_in, gz.at[d - 1], ctx=around(d)) for d in steps]
-    tok_in = gather(tok, x_all)
-    spreads = {"q": spread("q", wst.at[own_rows("q")])}
-    for n, at in zip("kv", lanes):
-        wb[at, :] = wst[own_rows(n), :]
-    for n in "qogud":
-        wb[block(n, mine), :] = wst[own_rows(n), :]
-    keep(tok, x_all)
-    keep(cot, c_all)
+    head_half, ff = plan["k"][1], plan["g"][1]
+    turn(HEAD_DIM)
+    kv_in, spreads = [], {}
+    for i, n in enumerate("kv"):
+        first = plan[n][2] + mine * HEAD_DIM
+        at = rows(first + half * head_half, head_half, 64)
+        wb[at, :] = turned[pl.ds(HEAD_DIM + i * head_half, head_half), :]
+        kv_in.append(send(wb.at[at], wb.at[at], ctx=near))
+        spreads[n] = spread_rows(at)
+    tok_in = [gather_start(tok, x_all, b) for b in both]
+    gains = [send(gain_in, gz.at[i], ctx=p) for i, p in enumerate((near, far, other))]
+    turn(0)
+    wb[block("q", mine), :] = turned[pl.ds(0, HEAD_DIM), :]
+    spreads["q"] = spread("q")
+    wb[block("o", mine), :] = out_rows[...]
     arrive(kv_in)
     for n in "kv":
-        spreads[n] = spread(n, wb.at[block(n, mine)])
-    for n in "ogud":
-        spreads[n] = spread(n, wst.at[own_rows(n)])
+        first = plan[n][2] + mine * HEAD_DIM
+        late = spread_rows(rows(first + (1 - half) * head_half, head_half, 64))
+        for early, more in zip(spreads[n], late):
+            early.extend(more)
+    spreads["o"] = spread("o")
     arrive(gains)
-    total = gain_in[...]
-    for d in steps:
-        total = total + gz[d - 1]
-    gsum[...] = total
+    gsum[...] = gain_in[...] + gz[0] + gz[1] + gz[2]
     gains = [send(gsum, gz_s.at[i], shard=p) for i, p in enumerate((sib, opp, dia))]
-    arrive(tok_in)
-    cot_in = gather(cot, c_all)
+    for first in range(2 * HEAD_DIM, turned.shape[0], HEAD_DIM):
+        turn(first)
+    wb[block("g", mine), :] = turned[pl.ds(2 * HEAD_DIM, ff), :]
+    wb[block("u", mine), :] = turned[pl.ds(2 * HEAD_DIM + ff, ff), :]
+    wb[block("d", mine), :] = down_rows[...]
+    tok_in = [gather_pass(x_all, b, tok_in[b]) for b in both]
     arrive(gains)
     gfull[...] = gsum[...] + gz_s[0] + gz_s[1] + gz_s[2]
     g_attn = gfull[0:1, :]
     g_mlp = gfull[1:2, :]
     g_query = gfull[2:3, :HEAD_DIM]
     g_key = gfull[2:3, HEAD_DIM : 2 * HEAD_DIM]
-
-    def norm_rows(i, carry):
-        b, j = i // ctx, i % ctx
-        x = x_all[b, j].astype(jnp.float32)
-        nx[b, j] = (x * rms_scale(x) * g_attn).astype(jnp.bfloat16)
-        return carry
-
-    lax.fori_loop(0, sequences * ctx, norm_rows, 0)
-
     passed = {}
-    for n in "qkv":
-        arrive([spreads[n][0]])
-        passed[n] = pass_on(n)
-    for n in "qkv":
-        arrive([spreads[n][1], passed[n]])
-
-    def attend(b, carry):
+
+    def pass_weights(names):
+        for n in names:
+            arrive(spreads[n][0])
+            passed[n] = pass_on(n)
+
+    def have_weights(names):
+        for n in names:
+            arrive(spreads[n][1] + [passed[n]])
+
+    pass_weights("qkv")
+
+    def norm_rows(b):
+        def one(j, carry):
+            x = x_all[b, j].astype(jnp.float32)
+            nx[b, j] = (x * rms_scale(x) * g_attn).astype(jnp.bfloat16)
+            return carry
+
+        lax.fori_loop(0, ctx, one, 0)
+
+    def attend(b):
         x = whole(nx, b)
         query = against_rows(x, matrix("q"))
         key = against_rows(x, matrix("k"))
         value = against_rows(x, matrix("v")).astype(jnp.bfloat16)
-        cos_b, sin_b, allowed = cosine[b], sine[b], mask[b] > 0.5
+        cos_b, sin_b = cosine[b], sine[b]
+        key_at = jnp.broadcast_to(pos[b : b + 1, :].astype(jnp.float32), (length, length))
+        key_doc = jnp.broadcast_to(seg[b : b + 1, :].astype(jnp.float32), (length, length))
+        allowed = (key_doc.T == key_doc) & (key_at <= key_at.T)
         for h in range(heads):
             at = slice(h * HEAD_DIM, (h + 1) * HEAD_DIM)
             q, k, v = query[:, at], key[:, at], value[:, at]
@@ -532,36 +578,39 @@
             p = exponent / jnp.sum(exponent, axis=-1, keepdims=True)
             prob[b, h] = p
             att[b, :, at] = plain(p.astype(jnp.bfloat16), v).astype(jnp.bfloat16)
-        return carry
-
-    lax.fori_loop(0, sequences, attend, 0)
-
-    arrive([spreads["o"][0]])
-    passed["o"] = pass_on("o")
-    arrive([spreads["o"][1], passed["o"]])
-
-    def project(b, carry):
+
+    out_part, cot_in = [], []
+    for b in both:
+        arrive(tok_in[b])
+        norm_rows(b)
+        if b == 0:
+            have_weights("qkv")
+        else:
+            cot_in = [gather_start(cot, c_all, i) for i in both]
+            for n in "gud":
+                spreads[n] = spread(n)
+        attend(b)
+        if b == 0:
+            pass_weights("o")
+            have_weights("o")
+        else:
+            out_part[0] = reduce_pass(part_a, got_a, 0, out_part[0])
         split(plain(att[b], matrix("o")), part_a, b)
-        return carry
-
-    lax.fori_loop(0, sequences, project, 0)
-    copies = scatter(part_a, got_a)
-    for n in "gud":
-        arrive([spreads[n][0]])
-        passed[n] = pass_on(n)
-    arrive(copies)
-    for b in range(sequences):
-        m = tok[b].astype(jnp.float32) + collect(part_a, got_a, b)
+        out_part.append(reduce_start(part_a, got_a, b))
+    out_part[1] = reduce_pass(part_a, got_a, 1, out_part[1])
+    first_parts = list(lent)
+    mid_in = []
+    for b in both:
+        m = tok[b].astype(jnp.float32) + reduce_end(part_a, got_a, b, out_part[b])
         mixed[b] = m
         own_mid[b] = (m * rms_scale(m) * g_mlp).astype(jnp.bfloat16)
-    mid_in = gather(own_mid, nm)
-    keep(own_mid, nm)
-    for n in "gud":
-        arrive([spreads[n][1], passed[n]])
-    arrive(cot_in)
-    arrive(mid_in)
-
-    def feed(b, carry):
+        mid_in.append(gather_start(own_mid, nm, b))
+        cot_in[b] = gather_pass(c_all, b, cot_in[b])
+    pass_weights("gud")
+    mid_in = [gather_pass(nm, b, mid_in[b]) for b in both]
+    have_weights("gud")
+
+    def feed(b):
         n, ct = whole(nm, b), whole(c_all, b)
         gate = against_rows(n, matrix("g"))
         up = against_rows(n, matrix("u"))
@@ -572,22 +621,13 @@
         d_up = (d_hidden * gate * sig).astype(jnp.bfloat16)
         dga[b], dup[b] = d_gate, d_up
         split(plain(d_gate, matrix("g")) + plain(d_up, matrix("u")), part_b, b)
-        return carry
-
-    lax.fori_loop(0, sequences, feed, 0)
-    mid_back = scatter(part_b, got_b)
-    for copy in copies:
-        copy.wait_send()
-
-    def leave(b, carry):
-        split(plain(hid[b], matrix("d")), part_a, b)
-        return carry
-
-    lax.fori_loop(0, sequences, leave, 0)
-    out_back = scatter(part_a, got_c)
-
-    def flat(ref):
-        return ref.reshape(sequences * length, ref.shape[-1])
+
+    mid_back = []
+    for b in both:
+        arrive(cot_in[b])
+        arrive(mid_in[b])
+        feed(b)
+        mid_back.append(reduce_start(part_b, got_b, b))
 
     def weigh(name, left, right):
         _, _, off, size = plan[name]
@@ -607,23 +647,23 @@
             shard=sib,
         )
 
+    def core_sum(name, at):
+        _, _, off, size = plan[name]
+        here = gb[rows(off + (core * 2 + at) * size, size, 64), :]
+        there = rk[rows(off // 2 + at * size, size, 64), :]
+        return here.astype(jnp.float32) + there.astype(jnp.float32)
+
     def drain_core(name, copy):
         _, _, off, size = plan[name]
         arrive([copy])
-        here = rows(off + theirs * size, size, 64)
-        there = rows(off // 2 + (1 - side) * size, size, 64)
-        total = gb[here, :].astype(jnp.float32) + rk[there, :].astype(jnp.float32)
         at = pl.ds(off // 4, size)
-        hs[at, :] = total.astype(jnp.bfloat16)
+        hs[at, :] = core_sum(name, 1 - side).astype(jnp.bfloat16)
         return send(hs.at[at], ry.at[at], shard=opp)
 
     def drain_side(name, copy):
         own, own_size, off, size = plan[name]
         arrive([copy])
-        here = rows(off + mine * size, size, 64)
-        there = rows(off // 2 + side * size, size, 64)
-        total = gb[here, :].astype(jnp.float32) + rk[there, :].astype(jnp.float32)
-        total = total + ry[pl.ds(off // 4, size), :].astype(jnp.float32)
+        total = core_sum(name, side) + ry[pl.ds(off // 4, size), :].astype(jnp.float32)
         total = total.astype(jnp.bfloat16)
         at = pl.ds(own, own_size)
         if own_size == size:
@@ -631,7 +671,7 @@
             return send(xo.at[at], rx.at[at], rep=1 - r)
         i = "kv".index(name)
         kvh[i] = total
-        return send(kvh.at[i, rows((1 - half) * own_size, own_size, 64)], kvr.at[i], ctx=partner)
+        return send(kvh.at[i, rows((1 - half) * own_size, own_size, 64)], kvr.at[i], ctx=near)
 
     def drain_pair(name, copy):
         own, own_size, _, _ = plan[name]
@@ -642,39 +682,57 @@
         xo[at, :] = (total + kvr[i].astype(jnp.float32)).astype(jnp.bfloat16)
         return send(xo.at[at], rx.at[at], rep=1 - r)
 
+    results = dict(zip("qkvogud", (grad_q, grad_k, grad_v, grad_o, grad_g, grad_u, grad_d)))
+
     def drain_rep(name, copy):
         at = own_rows(name)
         arrive([copy])
-        grad_w[at, :] = xo[at, :].astype(jnp.float32) + rx[at, :].astype(jnp.float32)
-
-    moving = {}
-    moving["d"] = weigh("d", hid, c_all)
-    moving["g"] = weigh("g", dga, nm)
-    moving["u"] = weigh("u", dup, nm)
+        total = xo[at, :].astype(jnp.float32) + rx[at, :].astype(jnp.float32)
+        out = results[name]
+        if name in "od":
+            out[...] = total
+            return
+        size = total.shape[0]
+        for first in range(0, size, HEAD_DIM):
+            piece = total[first : min(first + HEAD_DIM, size)]
+            count = piece.shape[0]
+            if count < HEAD_DIM:
+                piece = jnp.concatenate([piece] * (HEAD_DIM // count), axis=0)
+            out[:, first : first + count] = piece.T[:, :count]
 
     dgt[...] = jnp.zeros_like(dgt)
-    arrive(mid_back)
-    for b in range(sequences):
-        d_mid = collect(part_b, got_b, b)
+    res_in = []
+
+    def enter(b):
+        d_mid = reduce_end(part_b, got_b, b, mid_back[b])
         m = mixed[b]
         r_mid = rms_scale(m)
         dgt[1:2, :] += jnp.sum(d_mid * m * r_mid, axis=0, keepdims=True)
         d_resid = cot[b].astype(jnp.float32) + norm_backward(d_mid, m, r_mid, g_mlp)
         dres[b] = d_resid
         own_res[b] = d_resid.astype(jnp.bfloat16)
-    res_in = gather(own_res, res)
-    keep(own_res, res)
-    for n in "dgu":
-        moving[n] = drain_core(n, moving[n])
-    arrive(out_back)
-    for b in range(sequences):
-        block_out[b] = (mixed[b] + collect(part_a, got_c, b)).astype(jnp.bfloat16)
-    for copy in mid_back:
-        copy.wait_send()
-    arrive(res_in)
-    moving["o"] = weigh("o", att, res)
-
-    def attend_back(b, carry):
+        res_in.append(gather_start(own_res, res, b))
+
+    reclaim(first_parts)
+    moving = {}
+    moving["d"] = weigh("d", hid, c_all)
+    moving["g"] = weigh("g", dga, nm)
+    moving["d"] = drain_core("d", moving["d"])
+    mid_back[0] = reduce_pass(part_b, got_b, 0, mid_back[0])
+    moving["u"] = weigh("u", dup, nm)
+    mid_back[1] = reduce_pass(part_b, got_b, 1, mid_back[1])
+    second_parts = lent[len(first_parts) :]
+    enter(0)
+    moving["g"] = drain_core("g", moving["g"])
+    enter(1)
+    moving["u"] = drain_core("u", moving["u"])
+    for b in both:
+        split(plain(hid[b], matrix("d")), part_a, b)
+    res_in = [gather_pass(res, b, res_in[b]) for b in both]
+    out_back = [reduce_start(part_a, got_c, 0)]
+    reclaim(second_parts)
+
+    def attend_back(b):
         d_att = against_rows(whole(res, b), matrix("o")).astype(jnp.bfloat16)
         cos_b, sin_b = cosine[b], sine[b]
 
@@ -701,48 +759,59 @@
             dgt[2:3, HEAD_DIM : 2 * HEAD_DIM] += row_k
         d_in = plain(dqb[b], matrix("q")) + plain(dkb[b], matrix("k")) + plain(dvb[b], matrix("v"))
         split(d_in, part_b, b)
-        return carry
-
-    lax.fori_loop(0, sequences, attend_back, 0)
-    in_back = scatter(part_b, got_d)
+
+    arrive(res_in[0])
+    moving["d"] = drain_side("d", moving["d"])
+    attend_back(0)
+    in_back = [reduce_start(part_b, got_d, 0)]
+    out_back[0] = reduce_pass(part_a, got_c, 0, out_back[0])
+    arrive(res_in[1])
+    moving["o"] = weigh("o", att, res)
+    moving["g"] = drain_side("g", moving["g"])
+    moving["o"] = drain_core("o", moving["o"])
+    attend_back(1)
+    in_back.append(reduce_start(part_b, got_d, 1))
+    moving["k"] = weigh("k", dkb, nx)
+    in_back[0] = reduce_pass(part_b, got_d, 0, in_back[0])
+    moving["v"] = weigh("v", dvb, nx)
+    moving["k"] = drain_core("k", moving["k"])
     moving["q"] = weigh("q", dqb, nx)
-    moving["k"] = weigh("k", dkb, nx)
-    moving["v"] = weigh("v", dvb, nx)
-    for n in "dgu":
-        moving[n] = drain_side(n, moving[n])
-    for n in "okvq":
-        moving[n] = drain_core(n, moving[n])
-    arrive(in_back)
-    for b in range(sequences):
-        d_in = collect(part_b, got_d, b)
+    moving["v"] = drain_core("v", moving["v"])
+    moving["q"] = drain_core("q", moving["q"])
+    moving["u"] = drain_side("u", moving["u"])
+    in_back[1] = reduce_pass(part_b, got_d, 1, in_back[1])
+    out_back.append(reduce_start(part_a, got_c, 1))
+    moving["o"] = drain_side("o", moving["o"])
+    for b in both:
+        d_in = reduce_end(part_b, got_d, b, in_back[b])
         x = tok[b].astype(jnp.float32)
         r_in = rms_scale(x)
         dgt[0:1, :] += jnp.sum(d_in * x * r_in, axis=0, keepdims=True)
         grad_in[b] = dres[b] + norm_backward(d_in, x, r_in, g_attn)
-    gains = [send(dgt, dz.at[d - 1], ctx=around(d)) for d in steps]
-    for n in "okv":
-        moving[n] = drain_side(n, moving[n])
+    gains = [send(dgt, dz.at[i], ctx=p) for i, p in enumerate((near, far, other))]
+    moving["k"] = drain_side("k", moving["k"])
+    out_back[1] = reduce_pass(part_a, got_c, 1, out_back[1])
+    moving["v"] = drain_side("v", moving["v"])
+    drain_rep("d", moving["d"])
     arrive(gains)
-    total = dgt[...]
-    for d in steps:
-        total = total + dz[d - 1]
-    dsum[...] = total
+    dsum[...] = dgt[...] + dz[0] + dz[1] + dz[2]
     gains = [send(dsum, dz_s.at[i], shard=p) for i, p in enumerate((sib, opp, dia))]
     moving["q"] = drain_side("q", moving["q"])
-    for n in "dgu":
-        drain_rep(n, moving[n])
+    moving["k"] = drain_pair("k", moving["k"])
+    moving["v"] = drain_pair("v", moving["v"])
+    drain_rep("g", moving["g"])
     arrive(gains)
     dtot[...] = dsum[...] + dz_s[0] + dz_s[1] + dz_s[2]
     gains = [send(dtot, dz_x, rep=1 - r)]
-    for n in "kv":
-        moving[n] = drain_pair(n, moving[n])
-    for n in "oqkv":
+    for b in both:
+        total = mixed[b] + reduce_end(part_a, got_c, b, out_back[b])
+        block_out[b] = total.astype(jnp.bfloat16)
+    for n in "uoqkv":
         drain_rep(n, moving[n])
     arrive(gains)
     gain_out[...] = dtot[...] + dz_x[...]
-    waited = {id(copy) for copy in copies + mid_back}
     for copy in sends:
-        if id(copy) not in waited:
+        if not any(copy is late for late in returned):
             copy.wait_send()
 
 
@@ -767,18 +836,7 @@
     half = key_weight.shape[1]
     plan, own_total, full_total = row_plan(half, ff)
     heads = 4
-    stacked = jnp.concatenate(
-        [
-            w_query.T,
-            key_weight.T,
-            value_weight.T,
-            output_weight,
-            w_gate.T,
-            w_up.T,
-            w_down,
-        ],
-        axis=0,
-    )
+    columns = jnp.concatenate([w_query, key_weight, value_weight, w_gate, w_up], axis=1)
     count = norm_gains.shape[0]
     place = lax.axis_index("shard") * ctx + lax.axis_index("ctx")
     all_gains = width * 2 + 2 * HEAD_DIM
@@ -797,11 +855,6 @@
     cosine, sine = cosine[:, :, 0], sine[:, :, 0]
     cosine = jnp.concatenate([cosine, cosine], axis=-1)
     sine = jnp.concatenate([-sine, sine], axis=-1)
-    allowed = (
-        (segments[:, :, None] == segments[:, None, :])
-        & (positions[:, None, :] <= positions[:, :, None])
-    ).astype(jnp.float32)
-
     bf, f32 = jnp.bfloat16, jnp.float32
     gathered = pltpu.VMEM((sequences, ctx, span, width), bf)
     own_block = pltpu.VMEM((sequences, span, width), bf)
@@ -811,7 +864,7 @@
     head_lanes = pltpu.VMEM((sequences, length, heads * HEAD_DIM), bf)
     ff_lanes = pltpu.VMEM((sequences, length, heads * ff), bf)
     parts = pltpu.VMEM((ctx, sequences, span, width), bf)
-    got = pltpu.VMEM((ctx - 1, sequences, span, width), bf)
+    got = pltpu.VMEM((3, sequences, span, width), bf)
     tile = pltpu.VMEM((8, width), f32)
     tiles_c = pltpu.VMEM((ctx - 1, 8, width), f32)
     tiles_s = pltpu.VMEM((3, 8, width), f32)
@@ -821,16 +874,27 @@
 
     copies = 128
     vmem = pl.BlockSpec(memory_space=pltpu.VMEM)
-    block_out, grad_input, grads, gains_sum = pl.pallas_call(
+    outs = pl.pallas_call(
         functools.partial(layer_kernel, plan),
         out_shape=(
             jax.ShapeDtypeStruct(tokens.shape, bf),
             jax.ShapeDtypeStruct(tokens.shape, f32),
-            jax.ShapeDtypeStruct((own_total, width), f32),
+            *(
+                jax.ShapeDtypeStruct(weight.shape, f32)
+                for weight in (
+                    w_query,
+                    key_weight,
+                    value_weight,
+                    output_weight,
+                    w_gate,
+                    w_up,
+                    w_down,
+                )
+            ),
             jax.ShapeDtypeStruct((8, width), f32),
         ),
-        in_specs=[vmem] * 7,
-        out_specs=[vmem] * 4,
+        in_specs=[vmem] * 10,
+        out_specs=[vmem] * 10,
         scratch_shapes=[
             gathered,
             gathered,
@@ -839,6 +903,7 @@
             gathered,
             own_block,
             own_block,
+            row_buffer(columns.shape[1]),
             row_buffer(full_total),
             head_float,
             head_float,
@@ -885,32 +950,28 @@
         compiler_params=pltpu.CompilerParams(
             collective_id=0, has_side_effects=True, vmem_limit_bytes=67043328
         ),
-    )(tokens, cotangent, stacked, gain_rows, allowed, cosine, sine)
-
-    def part(name):
-        at, size = plan[name][:2]
-        return grads[at : at + size]
-
+    )(
+        tokens,
+        cotangent,
+        columns,
+        output_weight,
+        w_down,
+        gain_rows,
+        positions,
+        segments,
+        cosine,
+        sine,
+    )
+    gains_sum = outs[-1]
     flat = jnp.concatenate([gains_sum[0], gains_sum[2, : 2 * HEAD_DIM], gains_sum[1]])
-    return (
-        block_out,
-        grad_input,
-        part("q").T,
-        part("k").T,
-        part("v").T,
-        part("o"),
-        part("g").T,
-        part("u").T,
-        part("d"),
-        lax.dynamic_slice(flat, (place * count,), (count,)),
-    )
+    return (*outs[:-1], lax.dynamic_slice(flat, (place * count,), (count,)))
 
 
 def any_body(*arguments):
     tokens, w_query, key_weight, w_gate = (arguments[i] for i in (0, 4, 5, 8))
     ctx, shards = lax.axis_size("ctx"), lax.axis_size("shard")
     fits = w_query.shape[1] == HEAD_DIM and 2 * key_weight.shape[1] == HEAD_DIM
-    fits = fits and lax.axis_size("rep") == 2 and shards == 4 and ctx % 2 == 0
+    fits = fits and lax.axis_size("rep") == 2 and shards == 4 and ctx == 4
     fits = fits and w_gate.shape[1] % 64 == 0 and tokens.shape[1] % 16 == 0
     fits = fits and tokens.shape[0] * tokens.shape[1] * ctx <= 512
     if fits:

time: 277 us -> 208 us (0.75)
  Pallas kernels: 249 us -> 184 us
    pallas_call x1, Pallas kernels: 249 us -> 184 us  [whole_layer_body(): pl.pallas_call(functools.partial(layer_kernel, plan), out_shape=(jax.Shap...]
    unnamed x26 -> x31, local copies, waits for them, and re-layouts: 7.96 us -> 13.9 us
    slice x2 -> x0, local copies, waits for them, and re-layouts: 5.24 us -> none  [part(): return grads[at:at + size]]
where the time goes in v1:
time: 208 us; the launch traced here: 207 us
  Pallas kernels  184 us (88%)
  local copies, waits for them, and re-layouts  18.3 us (9%)
  other arithmetic  4.12 us (2%)
    pallas_call x1, Pallas kernels, whole_layer_body(): pl.pallas_call(functools.partial(layer_kernel, plan), out_shape=(jax.Shap...  184 us
    unnamed x31, local copies, waits for them, and re-layouts  13.9 us

profile of v1, /device:TPU:0, one launch (start us, length us, event | category | flops | bytes accessed | tf_op | source)
XLA Modules:
  0.0 207.2 jit_solution(7142941402938267037)
XLA Ops:
  0.6 0.0 copy-start.6
  0.7 0.7 convert_element_type.7
  1.4 0.7 convert_dynamic-update-slice_fusion
  2.2 0.6 reshape.30.gain_in
  2.8 0.0 copy-start.7
  2.8 1.1 copy.22
  3.9 1.1 copy.23
  5.0 1.2 copy.24
  6.2 0.0 copy-done.6
  6.2 0.2 copy.25
  6.5 0.0 copy-done.7
  6.5 2.1 %concatenate.15.columns = bf16[1024,640]{1,0:T(8,128)(2,1)} concatenate(bf16[1024,128]{1,0:T(8,128)(2,1)S(1)} %copy-done.7, bf16[1024,64]{1,0:T(8,128)(2,1)S(1)} %copy.22, bf16[1024,64]{1,0:T(8,128)(2,1)S(1)} %copy.23, bf16[1024,192]{1,0:T(8,128)(2,1)S(1)} %copy.24, bf16[1024,192]{1,0:T(8,128)(2,1)S(1)} %copy.25), dimensions={1} | concatenate | bytes 2621440 | tf_op jit(solution)/shard_map/concatenate | solution.py:839
  8.6 1.0 fusion
  9.6 1.0 pad_maximum_fusion
  10.5 184.0 %shard_map.195 = (bf16[2,64,1024]{2,1,0:T(8,128)(2,1)}, f32[2,64,1024]{2,1,0:T(8,128)}, f32[1024,128]{1,0:T(8,128)}, f32[1024,64]{1,0:T(8,128)}, f32[1024,64]{1,...) custom-call(bf16[2,64,1024]{2,1,0:T(8,128)(2,1)} %tok.1, ...), custom_call_target="tpu_custom_call" | custom-call | tf_op jit(solution)/shard_map/pallas_call | solution.py:877
  194.5 0.0 copy-start.1
  194.5 0.8 slice.22
  195.3 0.8 fusion.3
  196.2 0.6 fusion.2
  196.8 1.9 copy.26
  198.7 0.0 copy-start
  198.7 2.0 copy.27
  200.8 0.0 copy-done.1
  200.8 1.2 copy.28
  202.0 0.0 copy-done
  202.0 0.0 copy-start.8
  202.0 0.0 copy-start.5
  202.0 0.0 copy-start.4
  202.0 1.2 copy.29
  203.2 0.0 copy-done.8
  203.2 0.0 copy-start.3
  203.2 0.7 copy.36
  203.9 0.0 copy-done.5
  203.9 0.8 copy.37
  204.7 0.0 copy-done.4
  204.7 0.0 copy-start.2
  204.7 0.8 copy.38
  205.5 0.0 copy-done.3
  205.5 0.8 copy.39
  206.3 0.0 copy-done.2
  206.3 0.9 copy.40
  (6 shorter events, 0.0 us)
Async XLA Ops:
  0.6 5.6 %copy-start.6 = (bf16[1024,192]{0,1:T(8,128)(2,1)S(1)}, bf16[1024,192]{0,1:T(8,128)(2,1)}, u32[]{:S(2)}) copy-start(bf16[1024,192]{0,1:T(8,128)(2,1)} %param.21) | copy-start | bytes 1179652
  2.8 3.6 %copy-start.7 = (bf16[1024,128]{1,0:T(8,128)(2,1)S(1)}, bf16[1024,128]{1,0:T(8,128)(2,1)}, u32[]{:S(2)}) copy-start(bf16[1024,128]{1,0:T(8,128)(2,1)} %param.16) | copy-start | bytes 786436
  194.5 6.2 %copy-start.1 = (f32[1024,192]{1,0:T(8,128)S(1)}, f32[1024,192]{1,0:T(8,128)}, u32[]{:S(2)}) copy-start(f32[1024,192]{1,0:T(8,128)} %get-tuple-element.36) | copy-start | bytes 2359300
  198.7 3.2 %copy-start = (f32[1024,192]{1,0:T(8,128)S(1)}, f32[1024,192]{1,0:T(8,128)}, u32[]{:S(2)}) copy-start(f32[1024,192]{1,0:T(8,128)} %get-tuple-element.37) | copy-start | bytes 2359300
  202.0 1.2 copy-start.8
  202.0 1.9 copy-start.5
  202.0 2.7 %copy-start.4 = (f32[1024,128]{1,0:T(8,128)S(1)}, f32[1024,128]{1,0:T(8,128)}, u32[]{:S(2)}) copy-start(f32[1024,128]{1,0:T(8,128)} %get-tuple-element.61) | copy-start | bytes 1572868
  203.2 2.3 %copy-start.3 = (f32[128,1024]{1,0:T(8,128)S(1)}, f32[128,1024]{1,0:T(8,128)}, u32[]{:S(2)}) copy-start(f32[128,1024]{1,0:T(8,128)} %get-tuple-element.64) | copy-start | bytes 1572868
  204.7 1.6 copy-start.2

commit v2 on v1

--- a/solution.py
+++ b/solution.py
@@ -314,12 +314,22 @@
     return pl.ds(pl.multiple_of(start, step), size)
 
 
+def hand_over(*refs):
+    count = len(refs) // 2
+    for src, dst in zip(refs[:count], refs[count:]):
+        dst[...] = src[...]
+
+
 def layer_kernel(
     plan,
     tok,
     cot,
-    columns,
+    w_q,
+    k_rows,
+    v_rows,
     out_rows,
+    gate_rows,
+    up_rows,
     down_rows,
     gain_in,
     pos,
@@ -343,7 +353,6 @@
     res,
     own_mid,
     own_res,
-    turned,
     wb,
     qf,
     kf,
@@ -486,10 +495,6 @@
         for j in range(ctx):
             dst[j, b] = values_in[j * span : (j + 1) * span].astype(jnp.bfloat16)
 
-    def turn(first):
-        at = pl.ds(first, HEAD_DIM)
-        turned[at, :] = columns[:, at].astype(jnp.float32).T.astype(jnp.bfloat16)
-
     barrier = pltpu.get_barrier_semaphore()
     peers = [{"ctx": near}, {"ctx": far}, {"ctx": other}]
     peers += [{"shard": sib}, {"shard": opp}, {"shard": dia}, {"rep": 1 - r}]
@@ -497,21 +502,23 @@
         pl.semaphore_signal(barrier, inc=1, device_id=peer, device_id_type=MESH)
     pl.semaphore_wait(barrier, len(peers))
 
-    head_half, ff = plan["k"][1], plan["g"][1]
-    turn(HEAD_DIM)
+    head_half = plan["k"][1]
+    gains = [send(gain_in, gz.at[i], ctx=p) for i, p in enumerate((near, far, other))]
     kv_in, spreads = [], {}
-    for i, n in enumerate("kv"):
+    for n, src in zip("kv", (k_rows, v_rows)):
         first = plan[n][2] + mine * HEAD_DIM
         at = rows(first + half * head_half, head_half, 64)
-        wb[at, :] = turned[pl.ds(HEAD_DIM + i * head_half, head_half), :]
+        wb[at, :] = src[...]
         kv_in.append(send(wb.at[at], wb.at[at], ctx=near))
         spreads[n] = spread_rows(at)
     tok_in = [gather_start(tok, x_all, b) for b in both]
-    gains = [send(gain_in, gz.at[i], ctx=p) for i, p in enumerate((near, far, other))]
-    turn(0)
-    wb[block("q", mine), :] = turned[pl.ds(0, HEAD_DIM), :]
+    wb[block("q", mine), :] = w_q[...].astype(jnp.float32).T.astype(jnp.bfloat16)
+    for n, src in zip("ogud", (out_rows, gate_rows, up_rows, down_rows)):
+        wb[block(n, mine), :] = src[...]
+    arrive(gains)
+    gsum[...] = gain_in[...] + gz[0] + gz[1] + gz[2]
+    gains = [send(gsum, gz_s.at[i], shard=p) for i, p in enumerate((sib, opp, dia))]
     spreads["q"] = spread("q")
-    wb[block("o", mine), :] = out_rows[...]
     arrive(kv_in)
     for n in "kv":
         first = plan[n][2] + mine * HEAD_DIM
@@ -520,15 +527,6 @@
             early.extend(more)
     spreads["o"] = spread("o")
     arrive(gains)
-    gsum[...] = gain_in[...] + gz[0] + gz[1] + gz[2]
-    gains = [send(gsum, gz_s.at[i], shard=p) for i, p in enumerate((sib, opp, dia))]
-    for first in range(2 * HEAD_DIM, turned.shape[0], HEAD_DIM):
-        turn(first)
-    wb[block("g", mine), :] = turned[pl.ds(2 * HEAD_DIM, ff), :]
-    wb[block("u", mine), :] = turned[pl.ds(2 * HEAD_DIM + ff, ff), :]
-    wb[block("d", mine), :] = down_rows[...]
-    tok_in = [gather_pass(x_all, b, tok_in[b]) for b in both]
-    arrive(gains)
     gfull[...] = gsum[...] + gz_s[0] + gz_s[1] + gz_s[2]
     g_attn = gfull[0:1, :]
     g_mlp = gfull[1:2, :]
@@ -545,7 +543,10 @@
         for n in names:
             arrive(spreads[n][1] + [passed[n]])
 
+    tok_in[0] = gather_pass(x_all, 0, tok_in[0])
     pass_weights("qkv")
+    tok_in[1] = gather_pass(x_all, 1, tok_in[1])
+    cot_in = [gather_start(cot, c_all, 0)]
 
     def norm_rows(b):
         def one(j, carry):
@@ -579,14 +580,13 @@
             prob[b, h] = p
             att[b, :, at] = plain(p.astype(jnp.bfloat16), v).astype(jnp.bfloat16)
 
-    out_part, cot_in = [], []
+    out_part = []
     for b in both:
         arrive(tok_in[b])
         norm_rows(b)
         if b == 0:
             have_weights("qkv")
         else:
-            cot_in = [gather_start(cot, c_all, i) for i in both]
             for n in "gud":
                 spreads[n] = spread(n)
         attend(b)
@@ -597,6 +597,8 @@
             out_part[0] = reduce_pass(part_a, got_a, 0, out_part[0])
         split(plain(att[b], matrix("o")), part_a, b)
         out_part.append(reduce_start(part_a, got_a, b))
+        if b == 0:
+            cot_in.append(gather_start(cot, c_all, 1))
     out_part[1] = reduce_pass(part_a, got_a, 1, out_part[1])
     first_parts = list(lent)
     mid_in = []
@@ -689,16 +691,7 @@
         arrive([copy])
         total = xo[at, :].astype(jnp.float32) + rx[at, :].astype(jnp.float32)
         out = results[name]
-        if name in "od":
-            out[...] = total
-            return
-        size = total.shape[0]
-        for first in range(0, size, HEAD_DIM):
-            piece = total[first : min(first + HEAD_DIM, size)]
-            count = piece.shape[0]
-            if count < HEAD_DIM:
-                piece = jnp.concatenate([piece] * (HEAD_DIM // count), axis=0)
-            out[:, first : first + count] = piece.T[:, :count]
+        out[...] = total.T if name == "q" else total
 
     dgt[...] = jnp.zeros_like(dgt)
     res_in = []
@@ -720,16 +713,17 @@
     moving["d"] = drain_core("d", moving["d"])
     mid_back[0] = reduce_pass(part_b, got_b, 0, mid_back[0])
     moving["u"] = weigh("u", dup, nm)
+    moving["g"] = drain_core("g", moving["g"])
     mid_back[1] = reduce_pass(part_b, got_b, 1, mid_back[1])
     second_parts = lent[len(first_parts) :]
     enter(0)
-    moving["g"] = drain_core("g", moving["g"])
+    moving["u"] = drain_core("u", moving["u"])
     enter(1)
-    moving["u"] = drain_core("u", moving["u"])
+    moving["d"] = drain_side("d", moving["d"])
     for b in both:
         split(plain(hid[b], matrix("d")), part_a, b)
     res_in = [gather_pass(res, b, res_in[b]) for b in both]
-    out_back = [reduce_start(part_a, got_c, 0)]
+    out_back = [reduce_start(part_a, got_c, b) for b in both]
     reclaim(second_parts)
 
     def attend_back(b):
@@ -761,27 +755,27 @@
         split(d_in, part_b, b)
 
     arrive(res_in[0])
-    moving["d"] = drain_side("d", moving["d"])
+    moving["g"] = drain_side("g", moving["g"])
     attend_back(0)
     in_back = [reduce_start(part_b, got_d, 0)]
     out_back[0] = reduce_pass(part_a, got_c, 0, out_back[0])
     arrive(res_in[1])
     moving["o"] = weigh("o", att, res)
-    moving["g"] = drain_side("g", moving["g"])
+    moving["u"] = drain_side("u", moving["u"])
     moving["o"] = drain_core("o", moving["o"])
     attend_back(1)
     in_back.append(reduce_start(part_b, got_d, 1))
+    out_back[1] = reduce_pass(part_a, got_c, 1, out_back[1])
     moving["k"] = weigh("k", dkb, nx)
-    in_back[0] = reduce_pass(part_b, got_d, 0, in_back[0])
     moving["v"] = weigh("v", dvb, nx)
     moving["k"] = drain_core("k", moving["k"])
+    in_back[0] = reduce_pass(part_b, got_d, 0, in_back[0])
     moving["q"] = weigh("q", dqb, nx)
     moving["v"] = drain_core("v", moving["v"])
+    moving["o"] = drain_side("o", moving["o"])
     moving["q"] = drain_core("q", moving["q"])
-    moving["u"] = drain_side("u", moving["u"])
     in_back[1] = reduce_pass(part_b, got_d, 1, in_back[1])
-    out_back.append(reduce_start(part_a, got_c, 1))
-    moving["o"] = drain_side("o", moving["o"])
+    moving["k"] = drain_side("k", moving["k"])
     for b in both:
         d_in = reduce_end(part_b, got_d, b, in_back[b])
         x = tok[b].astype(jnp.float32)
@@ -789,16 +783,14 @@
         dgt[0:1, :] += jnp.sum(d_in * x * r_in, axis=0, keepdims=True)
         grad_in[b] = dres[b] + norm_backward(d_in, x, r_in, g_attn)
     gains = [send(dgt, dz.at[i], ctx=p) for i, p in enumerate((near, far, other))]
-    moving["k"] = drain_side("k", moving["k"])
-    out_back[1] = reduce_pass(part_a, got_c, 1, out_back[1])
     moving["v"] = drain_side("v", moving["v"])
-    drain_rep("d", moving["d"])
+    moving["k"] = drain_pair("k", moving["k"])
     arrive(gains)
     dsum[...] = dgt[...] + dz[0] + dz[1] + dz[2]
     gains = [send(dsum, dz_s.at[i], shard=p) for i, p in enumerate((sib, opp, dia))]
     moving["q"] = drain_side("q", moving["q"])
-    moving["k"] = drain_pair("k", moving["k"])
     moving["v"] = drain_pair("v", moving["v"])
+    drain_rep("d", moving["d"])
     drain_rep("g", moving["g"])
     arrive(gains)
     dtot[...] = dsum[...] + dz_s[0] + dz_s[1] + dz_s[2]
@@ -806,7 +798,7 @@
     for b in both:
         total = mixed[b] + reduce_end(part_a, got_c, b, out_back[b])
         block_out[b] = total.astype(jnp.bfloat16)
-    for n in "uoqkv":
+    for n in "uokqv":
         drain_rep(n, moving[n])
     arrive(gains)
     gain_out[...] = dtot[...] + dz_x[...]
@@ -836,7 +828,7 @@
     half = key_weight.shape[1]
     plan, own_total, full_total = row_plan(half, ff)
     heads = 4
-    columns = jnp.concatenate([w_query, key_weight, value_weight, w_gate, w_up], axis=1)
+    k_rows, v_rows, g_rows, u_rows = key_weight.T, value_weight.T, w_gate.T, w_up.T
     count = norm_gains.shape[0]
     place = lax.axis_index("shard") * ctx + lax.axis_index("ctx")
     all_gains = width * 2 + 2 * HEAD_DIM
@@ -883,17 +875,17 @@
                 jax.ShapeDtypeStruct(weight.shape, f32)
                 for weight in (
                     w_query,
-                    key_weight,
-                    value_weight,
+                    k_rows,
+                    v_rows,
                     output_weight,
-                    w_gate,
-                    w_up,
+                    g_rows,
+                    u_rows,
                     w_down,
                 )
             ),
             jax.ShapeDtypeStruct((8, width), f32),
         ),
-        in_specs=[vmem] * 10,
+        in_specs=[vmem] * 14,
         out_specs=[vmem] * 10,
         scratch_shapes=[
             gathered,
@@ -903,7 +895,6 @@
             gathered,
             own_block,
             own_block,
-            row_buffer(columns.shape[1]),
             row_buffer(full_total),
             head_float,
             head_float,
@@ -953,8 +944,12 @@
     )(
         tokens,
         cotangent,
-        columns,
+        w_query,
+        k_rows,
+        v_rows,
         output_weight,
+        g_rows,
+        u_rows,
         w_down,
         gain_rows,
         positions,
@@ -962,9 +957,16 @@
         cosine,
         sine,
     )
-    gains_sum = outs[-1]
+    outs = pl.pallas_call(
+        hand_over,
+        out_shape=[jax.ShapeDtypeStruct(out.shape, out.dtype) for out in outs],
+        in_specs=[vmem] * len(outs),
+        out_specs=[vmem] * len(outs),
+    )(*outs)
+    block_out, grad_input, d_q, d_k, d_v, d_o, d_g, d_u, d_d, gains_sum = outs
     flat = jnp.concatenate([gains_sum[0], gains_sum[2, : 2 * HEAD_DIM], gains_sum[1]])
-    return (*outs[:-1], lax.dynamic_slice(flat, (place * count,), (count,)))
+    own_gains = lax.dynamic_slice(flat, (place * count,), (count,))
+    return (block_out, grad_input, d_q, d_k.T, d_v.T, d_o, d_g.T, d_u.T, d_d, own_gains)
 
 
 def any_body(*arguments):

time: 208 us -> 189 us (0.909)
  local copies, waits for them, and re-layouts: 18.3 us -> 3.49 us
    unnamed x31 -> x4, local copies, waits for them, and re-layouts: 13.9 us -> 1.31 us
    pallas_call x1, Pallas kernels: 184 us -> 177 us  [whole_layer_body(): pl.pallas_call(functools.partial(layer_kernel, plan), out_shape=(jax.Shap...]
    pallas_call x0 -> x1, Pallas kernels: none -> 4.54 us  [whole_layer_body(): pl.pallas_call(hand_over, out_shape=[jax.ShapeDtypeStruct(out.shape, out....]
    concatenate x1 -> x0, local copies, waits for them, and re-layouts: 2.09 us -> none  [whole_layer_body(): jnp.concatenate([w_query, key_weight, value_weight, w_gate, w_up], axis=1)]
where the time goes in v2:
time: 189 us
  Pallas kernels  182 us (96%)
  local copies, waits for them, and re-layouts  3.49 us (2%)
  other arithmetic  2.74 us (1%)
    pallas_call x1, Pallas kernels, whole_layer_body(): pl.pallas_call(functools.partial(layer_kernel, plan), out_shape=(jax.Shap...  177 us
    pallas_call x1, Pallas kernels, whole_layer_body(): pl.pallas_call(hand_over, out_shape=[jax.ShapeDtypeStruct(out.shape, out....  4.54 us

profile of v2, /device:TPU:0, one launch (start us, length us, event | category | flops | bytes accessed | tf_op | source)
XLA Modules:
  0.0 188.6 jit_solution(9881232518885079670)
XLA Ops:
  0.6 0.0 copy-start
  0.7 0.7 copy-done
  1.3 0.0 copy-start.1
  1.3 0.7 copy-done.1
  2.0 0.1 convert_dynamic-update-slice_fusion
  2.1 0.6 reshape.30.gain_in
  2.7 1.0 fusion
  3.7 1.0 pad_maximum_fusion
  4.7 177.1 %shard_map.195 = (bf16[2,64,1024]{2,1,0:T(8,128)(2,1)}, f32[2,64,1024]{2,1,0:T(8,128)}, f32[1024,128]{1,0:T(8,128)}, f32[64,1024]{1,0:T(8,128)}, f32[64,1024]{1,...) custom-call(bf16[2,64,1024]{2,1,0:T(8,128)(2,1)} %tok.1, ...), custom_call_target="tpu_custom_call" | custom-call | tf_op jit(solution)/shard_map/pallas_call | solution.py:869
  181.9 4.5 %shard_map.196 = (bf16[2,64,1024]{2,1,0:T(8,128)(2,1)}, f32[2,64,1024]{2,1,0:T(8,128)}, f32[1024,128]{1,0:T(8,128)}, f32[64,1024]{1,0:T(8,128)}, f32[64,1024]{1,...) custom-call(bf16[2,64,1024]{2,1,0:T(8,128)(2,1)} %get-tuple-element., ...), custom_call_target="tpu_custom_call" | custom-call | tf_op jit(solution)/shard_map/pallas_call | solution.py:960
  186.4 0.7 slice.22
  187.1 0.8 fusion.3
  188.0 0.6 fusion.2
  (7 shorter events, 0.0 us)
Async XLA Ops:
  0.6 0.7 copy-start
  1.3 0.7 copy-start.1

commit v3 on v2

--- a/solution.py
+++ b/solution.py
@@ -776,6 +776,10 @@
     moving["q"] = drain_core("q", moving["q"])
     in_back[1] = reduce_pass(part_b, got_d, 1, in_back[1])
     moving["k"] = drain_side("k", moving["k"])
+    moving["v"] = drain_side("v", moving["v"])
+    moving["q"] = drain_side("q", moving["q"])
+    drain_rep("d", moving["d"])
+    drain_rep("g", moving["g"])
     for b in both:
         d_in = reduce_end(part_b, got_d, b, in_back[b])
         x = tok[b].astype(jnp.float32)
@@ -783,22 +787,19 @@
         dgt[0:1, :] += jnp.sum(d_in * x * r_in, axis=0, keepdims=True)
         grad_in[b] = dres[b] + norm_backward(d_in, x, r_in, g_attn)
     gains = [send(dgt, dz.at[i], ctx=p) for i, p in enumerate((near, far, other))]
-    moving["v"] = drain_side("v", moving["v"])
     moving["k"] = drain_pair("k", moving["k"])
+    moving["v"] = drain_pair("v", moving["v"])
     arrive(gains)
     dsum[...] = dgt[...] + dz[0] + dz[1] + dz[2]
     gains = [send(dsum, dz_s.at[i], shard=p) for i, p in enumerate((sib, opp, dia))]
-    moving["q"] = drain_side("q", moving["q"])
-    moving["v"] = drain_pair("v", moving["v"])
-    drain_rep("d", moving["d"])
-    drain_rep("g", moving["g"])
+    drain_rep("u", moving["u"])
     arrive(gains)
     dtot[...] = dsum[...] + dz_s[0] + dz_s[1] + dz_s[2]
     gains = [send(dtot, dz_x, rep=1 - r)]
     for b in both:
         total = mixed[b] + reduce_end(part_a, got_c, b, out_back[b])
         block_out[b] = total.astype(jnp.bfloat16)
-    for n in "uokqv":
+    for n in "oqkv":
         drain_rep(n, moving[n])
     arrive(gains)
     gain_out[...] = dtot[...] + dz_x[...]
@@ -843,10 +844,12 @@
             jnp.zeros((6 * width - 2 * HEAD_DIM,), jnp.float32),
         ]
     ).reshape(8, width)
-    cosine, sine = rope_tables(positions)
-    cosine, sine = cosine[:, :, 0], sine[:, :, 0]
-    cosine = jnp.concatenate([cosine, cosine], axis=-1)
-    sine = jnp.concatenate([-sine, sine], axis=-1)
+    lane = jnp.arange(HEAD_DIM)
+    power = (lane % (HEAD_DIM // 2)).astype(jnp.float32) * (2.0 / HEAD_DIM)
+    angle = positions.astype(jnp.float32)[..., None] * (1.0 / ROPE_BASE**power)
+    cosine = jnp.cos(angle)
+    sine = jnp.where(lane < HEAD_DIM // 2, -1.0, 1.0) * jnp.sin(angle)
+
     bf, f32 = jnp.bfloat16, jnp.float32
     gathered = pltpu.VMEM((sequences, ctx, span, width), bf)
     own_block = pltpu.VMEM((sequences, span, width), bf)

time: 189 us -> 189 us (level)
  no operation moved by 1% of the time
where the time goes in v3:
time: 189 us
  Pallas kernels  182 us (96%)
  local copies, waits for them, and re-layouts  3.51 us (2%)
  other arithmetic  2.55 us (1%)
    pallas_call x1, Pallas kernels, whole_layer_body(): pl.pallas_call(functools.partial(layer_kernel, plan), out_shape=(jax.Shap...  178 us
    pallas_call x1, Pallas kernels, whole_layer_body(): pl.pallas_call(hand_over, out_shape=[jax.ShapeDtypeStruct(out.shape, out....  4.54 us

profile of v3, /device:TPU:0, one launch (start us, length us, event | category | flops | bytes accessed | tf_op | source)
XLA Modules:
  0.0 189.1 jit_solution(1587018813293508011)
XLA Ops:
  0.7 0.0 copy-start
  0.7 0.7 copy-done
  1.4 0.0 copy-start.1
  1.4 0.7 copy-done.1
  2.0 0.1 convert_dynamic-update-slice_fusion
  2.1 0.6 reshape.42.gain_in
  2.8 1.8 fusion
  4.5 177.8 %shard_map.195 = (bf16[2,64,1024]{2,1,0:T(8,128)(2,1)}, f32[2,64,1024]{2,1,0:T(8,128)}, f32[1024,128]{1,0:T(8,128)}, f32[64,1024]{1,0:T(8,128)}, f32[64,1024]{1,...) custom-call(bf16[2,64,1024]{2,1,0:T(8,128)(2,1)} %tok.1, ...), custom_call_target="tpu_custom_call" | custom-call | tf_op jit(solution)/shard_map/pallas_call | solution.py:872
  182.4 4.5 %shard_map.196 = (bf16[2,64,1024]{2,1,0:T(8,128)(2,1)}, f32[2,64,1024]{2,1,0:T(8,128)}, f32[1024,128]{1,0:T(8,128)}, f32[64,1024]{1,0:T(8,128)}, f32[64,1024]{1,...) custom-call(bf16[2,64,1024]{2,1,0:T(8,128)(2,1)} %get-tuple-element., ...), custom_call_target="tpu_custom_call" | custom-call | tf_op jit(solution)/shard_map/pallas_call | solution.py:963
  186.9 0.7 slice.22
  187.6 0.8 fusion.7
  188.5 0.6 fusion.2
  (7 shorter events, 0.0 us)
Async XLA Ops:
  0.7 0.7 copy-start
  1.4 0.7 copy-start.1
